TPU v7x, 32 devices: a whole 2x2x4 slice. The times are simulated.
32 devices in a mesh: groups: 2 (over y), rx: 8 (over z, x), xl: 2 (over core).
Axes of the slice: x: 2, y: 2, z: 4, core: 2. Of those that a mesh axis runs over, the one named last changes fastest.
Arguments:
- source_traces: bfloat16 [4, 512, 2048], P(None, ('groups', 'rx', 'xl')), parts along dimension 1, may hold values from -6 to 6
- surface_filter: float32 [2, 1024], replicated, may hold values from -6 to 6
- records: bfloat16 [8192, 2048], P(('groups', 'rx', 'xl')), parts along dimension 0, may hold values from -6 to 6
- owners: int32 [8192], P(('groups', 'rx', 'xl')), parts along dimension 0, may hold values from 0 to 1, as said below
- aperture: int32 [64, 128], P(('groups', 'rx', 'xl')), parts along dimension 0, may hold values from 0 to 255, as said below
Outputs:
- multiples: bfloat16 [4, 64, 2048], P(None, ('groups', 'rx', 'xl')), parts along dimension 1
There are 2 independent parts, one for each index of `groups`. A program takes and returns all parts, laid end to end along the dimension named above; an argument that names none is the same for every part. Nothing has to cross between parts.
Inputs may be any that keep to these rules, and one draw needn't show every extreme that they name: owners holds the xl index of the destination, which has the same rx index as the record's device. Every owner receives exactly 256 records, at most 192 from one device, and in every draw some device sends exactly 192 records to one owner. `aperture`: the 128 indices of one output trace are distinct.
All inputs are finite; a program needn't handle non-finite values.
Results may differ from a plain program's by a relative error of at most 0.008.
Values may be sent and summed in bfloat16 or wider, within the bound.
No kernel may reach another device: no remote copies, remote signals or barrier semaphores. Data moves between devices by JAX's collectives and lax.ppermute only.
A program may use at most 128 MiB of HBM per device.

v0:
```python
import functools
import math

import jax
import jax.numpy as jnp
from jax import lax
from jax.experimental import pallas as pl
from jax.experimental.pallas import tpu as pltpu
from jax.sharding import PartitionSpec as P


F32, BF16, I32 = jnp.float32, jnp.bfloat16, jnp.int32
ROWS = 16
FORWARD_STEP = 32
INVERSE_STEP = 16


def turn(a, b):
    return a[0] * b[0] - a[1] * b[1], a[1] * b[0] + a[0] * b[1]


def angles(multiples, waves, samples):
    phase = ((multiples * waves) & (samples - 1)).astype(F32) * (2.0 * math.pi / samples)
    return jnp.cos(phase), jnp.sin(phase)


def row_of(pair, k):
    return pair[0][k : k + 1], pair[1][k : k + 1]


def build_forward(even, odd, fine):
    quarter = odd.shape[0]
    eighth = quarter // 2
    samples = 4 * quarter
    scale = 1.0 / math.sqrt(samples)
    first, ahead = [], []
    for k, rest in enumerate((0, 2, 1, 1)):
        row = lax.broadcasted_iota(I32, (8, eighth), 0)
        lane = lax.broadcasted_iota(I32, (8, eighth), 1)
        wave = 4 * (lane + (eighth if k == 3 else 0)) + rest
        columns = slice(k * eighth, (k + 1) * eighth)
        base = angles(row, wave, samples)
        jumps = angles(jnp.left_shift(8, jnp.minimum(row, 2)), wave, samples)
        base = (base[0] * scale, base[1] * scale)
        fine[0, 0:8, columns], fine[1, 0:8, columns] = base
        more = turn(base, row_of(jumps, 0))
        fine[0, 8:16, columns], fine[1, 8:16, columns] = more
        jump = row_of(jumps, 1)
        fine[0, 16:24, columns], fine[1, 16:24, columns] = turn(base, jump)
        fine[0, 24:32, columns], fine[1, 24:32, columns] = turn(more, jump)
        ahead.append(row_of(jumps, 2))
        first.append((jnp.ones((1, eighth), F32), jnp.zeros((1, eighth), F32)))

    def step(i, coarse):
        rows = pl.ds(i * FORWARD_STEP, FORWARD_STEP)
        for k in range(4):
            columns = slice(k * eighth, (k + 1) * eighth)
            cosine, sine = turn((fine[0, :, columns], fine[1, :, columns]), coarse[k])
            if k < 2:
                even[k, rows, :eighth] = cosine.astype(BF16)
                even[k, rows, eighth:] = (-sine).astype(BF16)
            else:
                start = (k - 2) * eighth
                odd[rows, start : start + eighth] = cosine.astype(BF16)
                odd[rows, quarter + start : quarter + start + eighth] = sine.astype(BF16)
        return [turn(a, b) for a, b in zip(coarse, ahead)]

    lax.fori_loop(0, quarter // FORWARD_STEP, step, first)


def forward_kernel(even, odd, fine):
    build_forward(even, odd, fine)


def inverse_kernel(even, odd, fine):
    quarter = odd.shape[0]
    eighth = quarter // 2
    samples = 4 * quarter
    scale = 1.0 / math.sqrt(samples // 2)
    row = lax.broadcasted_iota(I32, (8, quarter), 0)
    time = lax.broadcasted_iota(I32, (8, quarter), 1)
    base = angles(4 * row, time, samples)
    jumps = angles(jnp.where(row == 0, 32, jnp.where(row == 1, 64, row - 1)), time, samples)
    base = (base[0] * scale, base[1] * scale)
    base = (base, turn(base, row_of(jumps, 0)))
    for k, rest in enumerate((0, 2, 1)):
        for half in range(2):
            value = turn(base[half], row_of(jumps, 1 + rest)) if rest else base[half]
            rows = slice(8 * half, 8 * half + 8)
            fine[0, k, rows, :], fine[1, k, rows, :] = value
    ahead = row_of(jumps, 1)
    sign = 1.0 - 2.0 * (time[:1] & 1).astype(F32)

    def step(i, coarse):
        rows = pl.ds(i * INVERSE_STEP, INVERSE_STEP)
        later = pl.ds(eighth + i * INVERSE_STEP, INVERSE_STEP)
        for k in range(3):
            cosine, sine = turn((fine[0, k], fine[1, k]), coarse)
            if k < 2:
                even[k, rows, :] = cosine.astype(BF16)
                even[k, later, :] = (-sine).astype(BF16)
            else:
                odd[rows, :quarter] = cosine.astype(BF16)
                odd[rows, quarter:] = sine.astype(BF16)
                odd[later, :quarter] = (cosine * sign).astype(BF16)
                odd[later, quarter:] = (sine * sign).astype(BF16)
        return turn(coarse, ahead)

    first = (jnp.ones((1, quarter), F32), jnp.zeros((1, quarter), F32))
    lax.fori_loop(0, eighth // INVERSE_STEP, step, first)


def filters_kernel(filters, out):
    count = filters.shape[1]
    part = count // 4
    column = lax.broadcasted_iota(I32, (count, count), 1)
    source = jnp.where(
        column < 2 * part,
        jnp.where(column < part, 4 * column, 4 * (column - part) + 2),
        jnp.where(column < 3 * part, 4 * (column - 2 * part) + 1, 4 * (count - 1 - column) + 3),
    )
    move = (lax.broadcasted_iota(I32, (count, count), 0) == source).astype(F32).astype(BF16)
    left = filters[...]
    moved = jnp.zeros((2, count), F32)
    for _ in range(3):
        piece = left.astype(BF16)
        left = left - piece.astype(F32)
        moved = moved + jnp.dot(piece, move, preferred_element_type=F32)
    column = lax.broadcasted_iota(I32, (1, count), 1)
    out[0:1, :] = moved[0:1]
    out[1:2, :] = jnp.where(column < 3 * part, moved[1:2], -moved[1:2])


def split(x):
    quarter = x.shape[-1] // 4
    x0, x1, x2, x3 = (x[:, q * quarter : (q + 1) * quarter].astype(F32) for q in range(4))
    first, second = x0 + x2, x1 + x3
    return (
        (first + second).astype(BF16),
        (first - second).astype(BF16),
        (x0 - x2).astype(BF16),
        (x3 - x1).astype(BF16),
    )


def transform(parts, even, odd):
    rows = parts[0].shape[0]
    quarter = odd.shape[0]
    dot = functools.partial(jnp.dot, preferred_element_type=F32)
    both = dot(jnp.concatenate(parts[2:], axis=0), odd[...])
    return (
        dot(parts[0], even[0]),
        dot(parts[1], even[1]),
        both[:rows, :quarter] + both[rows:, quarter:],
        both[rows:, :quarter] - both[:rows, quarter:],
    )


def groups(samples):
    quarter, eighth = samples // 4, samples // 8
    return ((0, eighth, eighth), (quarter, eighth, eighth), (2 * quarter, quarter, quarter))


def setup_kernel(per_device, aper, place, *refs):
    sources, out = refs[:6], refs[6]
    data, owners, owners_other, entries, entries_other = refs[7:12]
    even, odd, fine, result, arriving, leaving = refs[12:]
    rec_dev, samples = sources[0].shape
    targets = (data.at[:rec_dev], data.at[rec_dev:], owners, owners_other, entries, entries_other)
    copies = [
        pltpu.make_async_copy(source, target, arriving.at[k])
        for k, (source, target) in enumerate(zip(sources, targets))
    ]
    for copy in copies:
        copy.start()
    build_forward(even, odd, fine)
    core = place[0]
    for copy in copies[2:]:
        copy.wait()
    slots = 2 * rec_dev
    outs = slots // aper
    out_dev = outs // 2
    earlier = (
        lax.broadcasted_iota(I32, (rec_dev, rec_dev), 0)
        < lax.broadcasted_iota(I32, (rec_dev, rec_dev), 1)
    ).astype(F32).astype(BF16)
    sides = (owners[...], owners_other[...])
    ranks, totals = [], []
    for owner in sides:
        mine = (owner == core).astype(F32)
        rank = jnp.dot(
            jnp.broadcast_to(mine, (8, rec_dev)).astype(BF16), earlier, preferred_element_type=F32
        )
        ranks.append(rank[:1])
        totals.append(jnp.sum(mine, axis=1, keepdims=True))
    position = lax.broadcasted_iota(I32, (1, rec_dev), 1)
    slot_row = lax.broadcasted_iota(I32, (slots, rec_dev), 0)
    picks = []
    for side in range(2):
        second = core != side
        before = (ranks[side] + jnp.where(second, totals[1 - side], 0.0)).astype(I32)
        index = position + jnp.where(second, rec_dev, 0)
        slot = jnp.where(sides[side] == core, before, rec_dev + index - before)
        picks.append((slot_row == slot).astype(F32).astype(BF16))
    picks = jnp.concatenate(picks, axis=1)
    trace = lax.broadcasted_iota(I32, (aper, aper), 0)
    trace = trace // per_device * (2 * per_device) + core * per_device + trace % per_device
    rows = []
    for r in range(outs):
        row = slice(r % out_dev, r % out_dev + 1)
        entry = (entries if r < out_dev else entries_other)[row, :]
        match = (trace == entry).astype(F32).astype(BF16)
        pick = picks[r * aper : (r + 1) * aper]
        rows.append(jnp.dot(match, pick, preferred_element_type=F32).astype(BF16))
    placed = jnp.concatenate(rows, axis=0)
    for copy in copies[:2]:
        copy.wait()
    routed = jnp.dot(placed, data[...], preferred_element_type=F32)
    first, sent = 0, []
    for k, block in enumerate(transform(split(routed), even, odd)):
        columns = slice(first, first + block.shape[1])
        first += block.shape[1]
        block = block.reshape(outs, aper // ROWS, ROWS, block.shape[1])
        for r in range(outs):
            result[:, r, :, columns] = block[r]
        copy = pltpu.make_async_copy(
            result.at[:, :, :, columns], out.at[:, :, :, columns], leaving.at[k]
        )
        copy.start()
        sent.append(copy)
    for copy in sent:
        copy.wait()


def ring_chunk(me, offset):
    place = jnp.where(me % 2 == 0, me // 2, 7 - me // 2)
    place = (place + offset) % 8
    return jnp.where(place < 4, 2 * place, 15 - 2 * place)


def sum_rows(values):
    row = lax.broadcasted_iota(I32, values[0].shape, 0)
    for shift in (4, 2, 1):
        upper = row % (2 * shift) < shift
        half = len(values) // 2
        joined = []
        for a, b in zip(values[:half], values[half:]):
            if shift == 4:
                rolled = pltpu.roll(jnp.where(upper, b, a), 4, 0)
            else:
                rolled = jnp.where(upper, pltpu.roll(a, 8 - shift, 0), pltpu.roll(b, shift, 0))
            joined.append(jnp.where(upper, a, b) + rolled)
        values = joined
    return values[0]


def halves_kernel(*refs):
    values, outs = refs[: len(refs) // 3], refs[len(refs) // 3 :]
    cut = outs[0].shape[0]
    for k, value in enumerate(values):
        outs[2 * k][...] = value[:cut]
        outs[2 * k + 1][...] = value[cut:]


def products_kernel(offsets, count, ringed, with_total, extra, place, *refs):
    pieces = refs[:count]
    even, odd, spectra = refs[count : count + 3]
    totals = refs[count + 3 : count + 3 + 2 * with_total]
    outs = refs[count + 3 + 2 * with_total + extra : -3]
    work, right, arriving = refs[-3:]
    copies = []
    for c, offset in enumerate(offsets):
        chunk = ring_chunk(place[0], offset) if ringed else offset
        copies.append(pltpu.make_async_copy(spectra.at[chunk], right.at[c], arriving.at[c]))
        copies[-1].start()
    samples = work.shape[1]
    number = right.shape[1]
    rows = work.shape[0] // len(offsets)
    sources = rows // ROWS
    data = jnp.concatenate([x[...].reshape(-1, samples) for x in pieces], axis=0)
    first = 0
    for block in transform(split(data), even, odd):
        work[:, first : first + block.shape[1]] = block
        first += block.shape[1]
    for copy in copies:
        copy.wait()
    if len(outs) > 2:
        outs[2][...] = jnp.zeros(outs[2].shape, F32)
    for start, distance, width in groups(samples):
        for block in range(width // 128):
            re = pl.ds(start + block * 128, 128)
            im = pl.ds(start + distance + block * 128, 128)
            sums = {}
            for c in range(len(offsets)):
                for r in range(number):
                    for h in range(ROWS // 8):
                        b_re, b_im = (right[c, r, 8 * h : 8 * h + 8, k] for k in (re, im))
                        for s in range(sources):
                            top = c * rows + s * ROWS + h * 8
                            a_re, a_im = work[top : top + 8, re], work[top : top + 8, im]
                            x = a_re * b_re - a_im * b_im
                            y = a_re * b_im + a_im * b_re
                            if (s, r) in sums:
                                x, y = x + sums[s, r][0], y + sums[s, r][1]
                            sums[s, r] = (x, y)
            share = number // 2
            for i in range(2):
                keys = [(s, i * share + r) for r in range(share) for s in range(sources)]
                for part, columns in enumerate((re, im)):
                    value = sum_rows([sums[key][part] for key in keys])
                    if with_total:
                        value = value + totals[i][:, columns]
                    outs[i][:, columns] = value


def finish_kernel(scale, filters, mine, arrived, even, odd, out):
    quarter = odd.shape[0]
    sources, out_dev, samples = out.shape
    raw = mine[...] + arrived[...]
    dot = functools.partial(jnp.dot, preferred_element_type=F32)
    filtered = []
    column = 0
    for start, distance, width in groups(samples):
        g_re = filters[0:1, column : column + width] * scale
        g_im = filters[1:2, column : column + width] * scale
        column += width
        x = raw[:, start : start + width]
        y = raw[:, start + distance : start + distance + width]
        filtered.append((g_re * x - g_im * y, g_re * y + g_im * x))
    a = dot(jnp.concatenate(filtered[0], axis=1).astype(BF16), even[0])
    b = dot(jnp.concatenate(filtered[1], axis=1).astype(BF16), even[1])
    both = dot(jnp.concatenate(filtered[2], axis=0).astype(BF16), odd[...])
    rows = raw.shape[0]
    h_re = both[:rows, :quarter] - both[rows:, quarter:]
    h_im = both[:rows, quarter:] + both[rows:, :quarter]
    plus, minus = a + b, a - b
    for q, value in enumerate((plus + h_re, minus - h_im, plus - h_re, minus + h_im)):
        value = value.reshape(out_dev, sources, quarter)
        for r in range(out_dev):
            out[:, r, q * quarter : (q + 1) * quarter] = value[r].astype(BF16)


def call(kernel, out_shape, kinds, scratch=(), limit=48, out_kinds=None):
    spaces = {"s": pltpu.SMEM, "v": pltpu.VMEM, "a": pl.ANY}
    specs = [pl.BlockSpec(memory_space=spaces[k]) for k in kinds]
    return pl.pallas_call(
        kernel,
        out_shape=out_shape,
        in_specs=specs,
        out_specs=[
            pl.BlockSpec(memory_space=spaces[k]) for k in out_kinds or "v" * len(out_shape)
        ],
        scratch_shapes=list(scratch),
        compiler_params=pltpu.CompilerParams(vmem_limit_bytes=limit << 20),
    )


def per_device(ring_size, source_traces, surface_filter, records, owners, aperture):
    sources, own_traces, samples = source_traces.shape
    out_dev, aper = aperture.shape
    rec_dev = records.shape[0]
    quarter = samples // 4
    struct = jax.ShapeDtypeStruct
    rx, xl = (lax.axis_index(axis).astype(I32).reshape(1) for axis in ("rx", "xl"))
    outs = 2 * out_dev
    chunks = aper // ROWS
    token = struct((8, 128), F32)

    def after(token, *values):
        return lax.optimization_barrier((*values, token))

    def swap(x):
        return lax.ppermute(x, "xl", [(0, 1), (1, 0)])

    owners = owners.reshape(1, -1)
    table_shapes = [struct((2, quarter, quarter), BF16), struct((quarter, 2 * quarter), BF16)]
    table_scratch = pltpu.VMEM((2, FORWARD_STEP, 2 * quarter), F32)

    def setup():
        spectra_shape = (chunks, outs, ROWS, samples)
        return call(
            functools.partial(setup_kernel, own_traces, aper),
            [struct(spectra_shape, F32)],
            "s" + "a" * 6,
            [
                pltpu.VMEM((2 * rec_dev, samples), BF16),
                *[pltpu.VMEM((1, rec_dev), I32)] * 2,
                *[pltpu.VMEM((out_dev, aper), I32)] * 2,
                *[pltpu.VMEM(shape.shape, BF16) for shape in table_shapes],
                table_scratch,
                pltpu.VMEM(spectra_shape, F32),
                pltpu.SemaphoreType.DMA((6,)),
                pltpu.SemaphoreType.DMA((4,)),
            ],
            61,
            "a",
        )(xl, records, swap(records), owners, swap(owners), aperture, swap(aperture))[0]

    def arrange(filters):
        return call(filters_kernel, [struct(filters.shape, F32)], "v")(filters)[0]

    def add(pieces, offsets, totals, ringed, extra=()):
        kernel = functools.partial(
            products_kernel, offsets, len(pieces), ringed, bool(totals), len(extra)
        )
        arguments = [*pieces, *tables, spectra, *totals, *extra]
        row_shape = struct((out_dev * sources, samples), F32)
        kinds = "s" + "v" * (len(pieces) + 2) + "a" + "v" * (len(totals) + len(extra))
        count = len(offsets)
        *result, done = call(
            kernel,
            [row_shape, row_shape, token],
            kinds,
            [
                pltpu.VMEM((count * sources * ROWS, samples), F32),
                pltpu.VMEM((count, outs, ROWS, samples), F32),
                pltpu.SemaphoreType.DMA((count,)),
            ],
        )(rx, *arguments)
        return result, done

    if ring_size == 8 and own_traces == ROWS:
        order = [0, 2, 4, 6, 7, 5, 3, 1]
        up = [(order[i], order[(i + 1) % 8]) for i in range(8)]
        down = [(b, a) for a, b in up]

        def step(a, b):
            return lax.ppermute(a, "rx", up), lax.ppermute(b, "rx", down)

        a1, b1 = step(source_traces, source_traces)
        *held, spectra = after(setup(), a1, b1)
        a2, b2 = step(*held)
        tables = call(forward_kernel, table_shapes, "", [table_scratch])()
        pieces = [source_traces, a1, b1]
        totals, done = add(pieces, [0, -1, 1], [], True)
        a2, b2, done = after(done, a2, b2)
        half = struct((sources // 2, own_traces, samples), BF16)
        up_first, up_second, down_first, down_second = call(halves_kernel, [half] * 4, "vv")(a2, b2)
        up_first, down_second = step(up_first, down_second)
        up_second, down_first = step(up_second, down_first)
        pieces = [up_first, up_second, down_first, down_second]
        totals, done = add([a2, b2], [-2, 2], totals, True, [done])
        up_first, down_second, surface_filter, done = after(
            done, up_first, down_second, surface_filter
        )
        last = step(up_first, down_second)
        filters = arrange(surface_filter)
        totals, _ = add(pieces, [-3, 3], totals, True, [done])
        (mine, theirs), _ = add(last, [4], totals, True)
    else:
        spectra = setup()
        tables = call(forward_kernel, table_shapes, "", [table_scratch])()
        gathered = lax.all_gather(source_traces, "rx", axis=1, tiled=True)
        parts = [gathered[:, k * ROWS : (k + 1) * ROWS] for k in range(chunks)]
        totals = []
        for k in range(0, chunks, 2):
            totals, _ = add(parts[k : k + 2], [k, k + 1], totals, False)
        mine, theirs = totals
        filters = arrange(surface_filter)

    fine = pltpu.VMEM((2, 3, INVERSE_STEP, quarter), F32)
    inverse = call(inverse_kernel, table_shapes, "", [fine])()
    return call(
        functools.partial(finish_kernel, 1.0 / math.sqrt(aper)),
        [struct((sources, out_dev, samples), BF16)],
        "vvvvv",
    )(filters, mine, swap(theirs), *inverse)[0]


def solution(mesh):
    in_specs = (
        P(None, ("groups", "rx", "xl"), None),
        P(),
        P(("groups", "rx", "xl"), None),
        P(("groups", "rx", "xl")),
        P(("groups", "rx", "xl"), None),
    )
    out_specs = P(None, ("groups", "rx", "xl"), None)
    return jax.shard_map(
        functools.partial(per_device, mesh.shape["rx"]),
        mesh=mesh,
        in_specs=in_specs,
        out_specs=out_specs,
        check_vma=False,
    )
```

profile of v0, /device:TPU:0, one launch (start us, length us, event | category | flops | bytes accessed | tf_op | source)
XLA Modules:
  0.0 40.4 jit_solution(14596225090742610735)
XLA Ops:
  0.0 0.0 copy-start
  0.0 0.5 %collective-permute-start.2 = (bf16[256,2048]{1,0:T(8,128)(2,1)}, bf16[256,2048]{1,0:T(8,128)(2,1)S(1)}, u32[]{:S(2)}, u32[]{:S(2)}) collective-permute-start(bf16[256,2048]{1,0:T(8,128)(2,1)} %refs_0_.2), channel_id=1, source_target_pairs={{0,1},{1,0},{2,3},{3,2},{4,5},{5,4},{6,7},{7,6},{8,9},{9,8},{10,11... | collective-permute-start | bytes 3145736 | tf_op jit(solution)/shard_map/ppermute | solution.py:373
  0.5 2.6 %collective-permute-start = (bf16[4,16,2048]{2,1,0:T(8,128)(2,1)}, bf16[4,16,2048]{2,1,0:T(8,128)(2,1)S(1)}, u32[]{:S(2)}, u32[]{:S(2)}) collective-permute-start(bf16[4,16,2048]{2,1,0:T(8,128)(2,1)} %refs_0_.3), channel_id=1, source_target_pairs={{0,4},{4,8},{8,12},{12,14},{14,10},{10,6},{6,2},{2,0},{1,5},{5,9},... | collective-permute-start | bytes 786440 | tf_op jit(solution)/shard_map/ppermute | solution.py:428
  3.1 0.0 collective-permute-start.1
  3.1 0.2 collective-permute-start.3
  3.3 0.3 collective-permute-start.4
  3.6 0.8 %collective-permute-done.3.refs_3_ = s32[1,256]{1,0:T(1,128)S(1)} collective-permute-done((s32[1,256]{1,0:T(1,128)}, s32[1,256]{1,0:T(1,128)S(1)}, u32[]{:S(2)}, u32[]{:S(2)}) %collective-permute-start.3) | collective-permute-done | bytes 1056 | tf_op jit(solution)/shard_map/ppermute | solution.py:373
  4.4 0.0 copy-start.3
  4.4 0.2 collective-permute-done.4.refs_5_
  4.6 0.0 copy-start.4
  4.6 0.0 collective-permute-done.2.refs_1_
  4.6 0.0 copy-start.2
  4.6 0.4 copy-done.3
  5.0 0.2 copy-done.4
  5.2 0.4 %copy-done.2 = bf16[256,2048]{1,0:T(8,128)(2,1)} copy-done((bf16[256,2048]{1,0:T(8,128)(2,1)}, bf16[256,2048]{1,0:T(8,128)(2,1)S(1)}, u32[]{:S(2)}) %copy-start.2) | copy-done | bytes 1048600
  5.6 6.6 %shard_map.55.refs_5_.refs_4_.refs_6_ = f32[8,4,16,2048]{3,2,1,0:T(8,128)} custom-call(s32[1]{0:T(128)} %bitcast.place, bf16[256,2048]{1,0:T(8,128)(2,1)} %refs_0_.2, bf16[256,2048]{1,0:T(8,128)(2,1)} %copy-done.2, s32[1,256]{1,0:T(1,128)} %bitcast.4, s32[1,256]{1,0:T(1,128)} %copy-done.3, s32[2,128]{1,0:T(2,128)} %refs_4_.1, s32[2,128]{1,0:T(2,128)} %copy-done.4), custom_call_target="tpu_custom_call" | custom-call | tf_op jit(solution)/shard_map/pallas_call | solution.py:381
  12.3 0.0 collective-permute-done.refs_1_
  12.3 0.0 collective-permute-done.1.refs_2_
  12.3 2.1 %collective-permute-start.5 = (bf16[4,16,2048]{2,1,0:T(8,128)(2,1)S(1)}, bf16[4,16,2048]{2,1,0:T(8,128)(2,1)S(1)}, u32[]{:S(2)}, u32[]{:S(2)}) collective-permute-start(bf16[4,16,2048]{2,1,0:T(8,128)(2,1)S(1)} %collective-permute-done.refs_1_), channel_id=1, source_target_pairs={{0,4},{4,8},{8,12},{12,14},{14,10},{10,6},{6,2},{2,0},{1,5},{5,9},... | collective-permute-start | bytes 786440 | tf_op jit(solution)/shard_map/ppermute | solution.py:428
  14.4 0.0 collective-permute-start.6
  14.4 1.0 %shard_map.56 = (bf16[2,512,512]{2,1,0:T(8,128)(2,1)S(1)}, bf16[512,1024]{1,0:T(8,128)(2,1)S(1)}) custom-call(), custom_call_target="tpu_custom_call" | custom-call | tf_op jit(solution)/shard_map/pallas_call | solution.py:433
  15.4 0.0 copy-done
  15.4 2.8 %shard_map.57 = (f32[8,2048]{1,0:T(8,128)S(1)}, f32[8,2048]{1,0:T(8,128)S(1)}, f32[8,128]{1,0:T(8,128)S(1)}) custom-call(s32[1]{0:T(128)} %bitcast.2.place, bf16[4,16,2048]{2,1,0:T(8,128)(2,1)S(1)} %copy-done, bf16[4,16,2048]{2,1,0:T(8,128)(2,1)S(1)} %collective-permute-done.refs_1_, bf16[4,16,2048]{2,1,0:T(8,128)(2,1)S(1)} %collective-permute-done.1.refs_2_, ...), custom_call_target="tpu_custom_call" | custom-call | tf_op jit(solution)/shard_map/pallas_call | solution.py:410
  18.2 2.9 %collective-permute-done.5.refs_0_ = bf16[4,16,2048]{2,1,0:T(8,128)(2,1)S(1)} collective-permute-done((bf16[4,16,2048]{2,1,0:T(8,128)(2,1)S(1)}, bf16[4,16,2048]{2,1,0:T(8,128)(2,1)S(1)}, u32[]{:S(2)}, u32[]{:S(2)}) %collective-permute-start.5) | collective-permute-done | bytes 262176 | tf_op jit(solution)/shard_map/ppermute | solution.py:428
  21.1 1.5 %collective-permute-done.6.refs_1_ = bf16[4,16,2048]{2,1,0:T(8,128)(2,1)S(1)} collective-permute-done((bf16[4,16,2048]{2,1,0:T(8,128)(2,1)S(1)}, bf16[4,16,2048]{2,1,0:T(8,128)(2,1)S(1)}, u32[]{:S(2)}, u32[]{:S(2)}) %collective-permute-start.6) | collective-permute-done | bytes 262176 | tf_op jit(solution)/shard_map/ppermute | solution.py:428
  22.7 1.6 %collective-permute-start.7 = (bf16[2,16,2048]{2,1,0:T(8,128)(2,1)S(1)}, bf16[2,16,2048]{2,1,0:T(8,128)(2,1)S(1)}, u32[]{:S(2)}, u32[]{:S(2)}) collective-permute-start(bf16[2,16,2048]{2,1,0:T(8,128)(2,1)S(1)} %get-tuple-element.41), channel_id=1, source_target_pairs={{0,4},{4,8},{8,12},{12,14},{14,10},{10,6},{6,2},{2,0},{1,5},{5,9},... | collective-permute-start | bytes 393224 | tf_op jit(solution)/shard_map/ppermute | solution.py:428
  24.3 0.5 %collective-permute-start.8 = (bf16[2,16,2048]{2,1,0:T(8,128)(2,1)S(1)}, bf16[2,16,2048]{2,1,0:T(8,128)(2,1)S(1)}, u32[]{:S(2)}, u32[]{:S(2)}) collective-permute-start(bf16[2,16,2048]{2,1,0:T(8,128)(2,1)S(1)} %get-tuple-element.42), channel_id=1, source_target_pairs={{4,0},{8,4},{12,8},{14,12},{10,14},{6,10},{2,6},{0,2},{5,1},{9,5},... | collective-permute-start | bytes 393224 | tf_op jit(solution)/shard_map/ppermute | solution.py:428
  24.8 1.6 %collective-permute-start.11 = (bf16[2,16,2048]{2,1,0:T(8,128)(2,1)S(1)}, bf16[2,16,2048]{2,1,0:T(8,128)(2,1)S(1)}, u32[]{:S(2)}, u32[]{:S(2)}) collective-permute-start(bf16[2,16,2048]{2,1,0:T(8,128)(2,1)S(1)} %get-tuple-element.50), channel_id=1, source_target_pairs={{0,4},{4,8},{8,12},{12,14},{14,10},{10,6},{6,2},{2,0},{1,5},{5,9},... | collective-permute-start | bytes 393224 | tf_op jit(solution)/shard_map/ppermute | solution.py:428
  26.3 0.5 %collective-permute-start.12 = (bf16[2,16,2048]{2,1,0:T(8,128)(2,1)S(1)}, bf16[2,16,2048]{2,1,0:T(8,128)(2,1)S(1)}, u32[]{:S(2)}, u32[]{:S(2)}) collective-permute-start(bf16[2,16,2048]{2,1,0:T(8,128)(2,1)S(1)} %get-tuple-element.51), channel_id=1, source_target_pairs={{4,0},{8,4},{12,8},{14,12},{10,14},{6,10},{2,6},{0,2},{5,1},{9,5},... | collective-permute-start | bytes 393224 | tf_op jit(solution)/shard_map/ppermute | solution.py:428
  26.8 2.3 %shard_map.59 = (f32[8,2048]{1,0:T(8,128)S(1)}, f32[8,2048]{1,0:T(8,128)S(1)}, f32[8,128]{1,0:T(8,128)S(1)}) custom-call(s32[1]{0:T(128)} %bitcast.2.place, bf16[4,16,2048]{2,1,0:T(8,128)(2,1)S(1)} %collective-permute-done.5.refs_0_, bf16[4,16,2048]{2,1,0:T(8,128)(2,1)S(1)} %collective-permute-done.6.refs_1_, ...), custom_call_target="tpu_custom_call" | custom-call | tf_op jit(solution)/shard_map/pallas_call | solution.py:410
  29.1 0.0 collective-permute-done.7.refs_0_
  29.1 1.0 %collective-permute-done.8.refs_3_ = bf16[2,16,2048]{2,1,0:T(8,128)(2,1)S(1)} collective-permute-done((bf16[2,16,2048]{2,1,0:T(8,128)(2,1)S(1)}, bf16[2,16,2048]{2,1,0:T(8,128)(2,1)S(1)}, u32[]{:S(2)}, u32[]{:S(2)}) %collective-permute-start.8) | collective-permute-done | bytes 131104 | tf_op jit(solution)/shard_map/ppermute | solution.py:428
  30.2 0.4 collective-permute-start.10
  30.5 1.6 %collective-permute-start.9 = (bf16[2,16,2048]{2,1,0:T(8,128)(2,1)S(1)}, bf16[2,16,2048]{2,1,0:T(8,128)(2,1)S(1)}, u32[]{:S(2)}, u32[]{:S(2)}) collective-permute-start(bf16[2,16,2048]{2,1,0:T(8,128)(2,1)S(1)} %collective-permute-done.7.refs_0_), channel_id=1, source_target_pairs={{0,4},{4,8},{8,12},{12,14},{14,10},{10,6},{6,2},{2,0},{1,5},{5,9},... | collective-permute-start | bytes 393224 | tf_op jit(solution)/shard_map/ppermute | solution.py:428
  32.2 0.0 collective-permute-done.11.refs_1_
  32.2 0.7 %collective-permute-done.12.refs_2_ = bf16[2,16,2048]{2,1,0:T(8,128)(2,1)S(1)} collective-permute-done((bf16[2,16,2048]{2,1,0:T(8,128)(2,1)S(1)}, bf16[2,16,2048]{2,1,0:T(8,128)(2,1)S(1)}, u32[]{:S(2)}, u32[]{:S(2)}) %collective-permute-start.12) | collective-permute-done | bytes 131104 | tf_op jit(solution)/shard_map/ppermute | solution.py:428
  32.9 2.3 %shard_map.61 = (f32[8,2048]{1,0:T(8,128)S(1)}, f32[8,2048]{1,0:T(8,128)S(1)}, f32[8,128]{1,0:T(8,128)}) custom-call(s32[1]{0:T(128)} %bitcast.2.place, bf16[2,16,2048]{2,1,0:T(8,128)(2,1)S(1)} %collective-permute-done.7.refs_0_, bf16[2,16,2048]{2,1,0:T(8,128)(2,1)S(1)} %collective-permute-done.11.refs_1_, ...), custom_call_target="tpu_custom_call" | custom-call | tf_op jit(solution)/shard_map/pallas_call | solution.py:410
  35.2 0.0 copy-start.1
  35.2 0.0 collective-permute-done.10.refs_1_
  35.2 0.3 collective-permute-done.9.refs_0_
  35.5 2.0 %shard_map.62 = (f32[8,2048]{1,0:T(8,128)S(1)}, f32[8,2048]{1,0:T(8,128)S(1)}, f32[8,128]{1,0:T(8,128)}) custom-call(s32[1]{0:T(128)} %bitcast.2.place, bf16[2,16,2048]{2,1,0:T(8,128)(2,1)S(1)} %collective-permute-done.9.refs_0_, bf16[2,16,2048]{2,1,0:T(8,128)(2,1)S(1)} %collective-permute-done.10.refs_1_, ...), custom_call_target="tpu_custom_call" | custom-call | tf_op jit(solution)/shard_map/pallas_call | solution.py:410
  37.5 0.1 collective-permute-start.13
  37.6 0.7 %shard_map.63 = (bf16[2,512,512]{2,1,0:T(8,128)(2,1)S(1)}, bf16[512,1024]{1,0:T(8,128)(2,1)S(1)}) custom-call(), custom_call_target="tpu_custom_call" | custom-call | tf_op jit(solution)/shard_map/pallas_call | solution.py:462
  38.3 0.0 copy-done.1
  38.3 1.1 %shard_map.60.filters = f32[2,1024]{1,0:T(2,128)S(1)} custom-call(f32[2,1024]{1,0:T(2,128)S(1)} %copy-done.1), custom_call_target="tpu_custom_call" | custom-call | tf_op jit(solution)/shard_map/pallas_call | solution.py:400
  39.4 0.0 collective-permute-done.13.arrived
  39.4 1.0 %shard_map.64 = bf16[4,2,2048]{2,1,0:T(2,128)(2,1)} custom-call(f32[2,1024]{1,0:T(2,128)S(1)} %shard_map.60.filters, f32[8,2048]{1,0:T(8,128)S(1)} %get-tuple-element.57.mine, f32[8,2048]{1,0:T(8,128)S(1)} %collective-permute-done.13.arrived, bf16[2,512,512]{2,1,0:T(8,128)(2,1)S(1)} %get-tuple-element.59.even, bf16[512,1024]{1,0:T(8,128)(2,1)S(1)} %get-tuple-element.60.odd), custom_call_target="tpu_custom_call" | custom-call | tf_op jit(solution)/shard_map/pallas_call | solution.py:463
  (1 shorter events, 0.0 us)
Async XLA Ops:
  0.0 15.4 %copy-start = (bf16[4,16,2048]{2,1,0:T(8,128)(2,1)S(1)}, bf16[4,16,2048]{2,1,0:T(8,128)(2,1)}, u32[]{:S(2)}) copy-start(bf16[4,16,2048]{2,1,0:T(8,128)(2,1)} %refs_0_.3) | copy-start | bytes 786436
  0.0 4.6 %collective-permute-start.2 = (bf16[256,2048]{1,0:T(8,128)(2,1)}, bf16[256,2048]{1,0:T(8,128)(2,1)S(1)}, u32[]{:S(2)}, u32[]{:S(2)}) collective-permute-start(bf16[256,2048]{1,0:T(8,128)(2,1)} %refs_0_.2), channel_id=1, source_target_pairs={{0,1},{1,0},{2,3},{3,2},{4,5},{5,4},{6,7},{7,6},{8,9},{9,8},{10,11... | collective-permute-start | bytes 3145736 | tf_op jit(solution)/shard_map/ppermute | solution.py:373
  0.5 11.8 %collective-permute-start = (bf16[4,16,2048]{2,1,0:T(8,128)(2,1)}, bf16[4,16,2048]{2,1,0:T(8,128)(2,1)S(1)}, u32[]{:S(2)}, u32[]{:S(2)}) collective-permute-start(bf16[4,16,2048]{2,1,0:T(8,128)(2,1)} %refs_0_.3), channel_id=1, source_target_pairs={{0,4},{4,8},{8,12},{12,14},{14,10},{10,6},{6,2},{2,0},{1,5},{5,9},... | collective-permute-start | bytes 786440 | tf_op jit(solution)/shard_map/ppermute | solution.py:428
  3.1 9.2 %collective-permute-start.1 = (bf16[4,16,2048]{2,1,0:T(8,128)(2,1)}, bf16[4,16,2048]{2,1,0:T(8,128)(2,1)S(1)}, u32[]{:S(2)}, u32[]{:S(2)}) collective-permute-start(bf16[4,16,2048]{2,1,0:T(8,128)(2,1)} %refs_0_.3), channel_id=1, source_target_pairs={{4,0},{8,4},{12,8},{14,12},{10,14},{6,10},{2,6},{0,2},{5,1},{9,5},... | collective-permute-start | bytes 786440 | tf_op jit(solution)/shard_map/ppermute | solution.py:428
  3.1 1.4 %collective-permute-start.3 = (s32[1,256]{1,0:T(1,128)}, s32[1,256]{1,0:T(1,128)S(1)}, u32[]{:S(2)}, u32[]{:S(2)}) collective-permute-start(s32[1,256]{1,0:T(1,128)} %bitcast.3), channel_id=1, source_target_pairs={{0,1},{1,0},{2,3},{3,2},{4,5},{5,4},{6,7},{7,6},{8,9},{9,8},{10,11... | collective-permute-start | bytes 3080 | tf_op jit(solution)/shard_map/ppermute | solution.py:373
  3.3 1.4 %collective-permute-start.4 = (s32[2,128]{1,0:T(2,128)}, s32[2,128]{1,0:T(2,128)S(1)}, u32[]{:S(2)}, u32[]{:S(2)}) collective-permute-start(s32[2,128]{1,0:T(2,128)} %refs_4_.1), channel_id=1, source_target_pairs={{0,1},{1,0},{2,3},{3,2},{4,5},{5,4},{6,7},{7,6},{8,9},{9,8},{10,11... | collective-permute-start | bytes 3080 | tf_op jit(solution)/shard_map/ppermute | solution.py:373
  4.4 0.6 %copy-start.3 = (s32[1,256]{1,0:T(1,128)}, s32[1,256]{1,0:T(1,128)S(1)}, u32[]{:S(2)}) copy-start(s32[1,256]{1,0:T(1,128)S(1)} %collective-permute-done.3.refs_3_) | copy-start | bytes 3076
  4.6 0.6 %copy-start.4 = (s32[2,128]{1,0:T(2,128)}, s32[2,128]{1,0:T(2,128)S(1)}, u32[]{:S(2)}) copy-start(s32[2,128]{1,0:T(2,128)S(1)} %collective-permute-done.4.refs_5_) | copy-start | bytes 3076
  4.6 1.0 %copy-start.2 = (bf16[256,2048]{1,0:T(8,128)(2,1)}, bf16[256,2048]{1,0:T(8,128)(2,1)S(1)}, u32[]{:S(2)}) copy-start(bf16[256,2048]{1,0:T(8,128)(2,1)S(1)} %collective-permute-done.2.refs_1_) | copy-start | bytes 3145732
  12.3 8.8 %collective-permute-start.5 = (bf16[4,16,2048]{2,1,0:T(8,128)(2,1)S(1)}, bf16[4,16,2048]{2,1,0:T(8,128)(2,1)S(1)}, u32[]{:S(2)}, u32[]{:S(2)}) collective-permute-start(bf16[4,16,2048]{2,1,0:T(8,128)(2,1)S(1)} %collective-permute-done.refs_1_), channel_id=1, source_target_pairs={{0,4},{4,8},{8,12},{12,14},{14,10},{10,6},{6,2},{2,0},{1,5},{5,9},... | collective-permute-start | bytes 786440 | tf_op jit(solution)/shard_map/ppermute | solution.py:428
  14.4 8.2 %collective-permute-start.6 = (bf16[4,16,2048]{2,1,0:T(8,128)(2,1)S(1)}, bf16[4,16,2048]{2,1,0:T(8,128)(2,1)S(1)}, u32[]{:S(2)}, u32[]{:S(2)}) collective-permute-start(bf16[4,16,2048]{2,1,0:T(8,128)(2,1)S(1)} %collective-permute-done.1.refs_2_), channel_id=1, source_target_pairs={{4,0},{8,4},{12,8},{14,12},{10,14},{6,10},{2,6},{0,2},{5,1},{9,5},... | collective-permute-start | bytes 786440 | tf_op jit(solution)/shard_map/ppermute | solution.py:428
  22.7 6.5 %collective-permute-start.7 = (bf16[2,16,2048]{2,1,0:T(8,128)(2,1)S(1)}, bf16[2,16,2048]{2,1,0:T(8,128)(2,1)S(1)}, u32[]{:S(2)}, u32[]{:S(2)}) collective-permute-start(bf16[2,16,2048]{2,1,0:T(8,128)(2,1)S(1)} %get-tuple-element.41), channel_id=1, source_target_pairs={{0,4},{4,8},{8,12},{12,14},{14,10},{10,6},{6,2},{2,0},{1,5},{5,9},... | collective-permute-start | bytes 393224 | tf_op jit(solution)/shard_map/ppermute | solution.py:428
  24.3 5.9 %collective-permute-start.8 = (bf16[2,16,2048]{2,1,0:T(8,128)(2,1)S(1)}, bf16[2,16,2048]{2,1,0:T(8,128)(2,1)S(1)}, u32[]{:S(2)}, u32[]{:S(2)}) collective-permute-start(bf16[2,16,2048]{2,1,0:T(8,128)(2,1)S(1)} %get-tuple-element.42), channel_id=1, source_target_pairs={{4,0},{8,4},{12,8},{14,12},{10,14},{6,10},{2,6},{0,2},{5,1},{9,5},... | collective-permute-start | bytes 393224 | tf_op jit(solution)/shard_map/ppermute | solution.py:428
  24.8 7.4 %collective-permute-start.11 = (bf16[2,16,2048]{2,1,0:T(8,128)(2,1)S(1)}, bf16[2,16,2048]{2,1,0:T(8,128)(2,1)S(1)}, u32[]{:S(2)}, u32[]{:S(2)}) collective-permute-start(bf16[2,16,2048]{2,1,0:T(8,128)(2,1)S(1)} %get-tuple-element.50), channel_id=1, source_target_pairs={{0,4},{4,8},{8,12},{12,14},{14,10},{10,6},{6,2},{2,0},{1,5},{5,9},... | collective-permute-start | bytes 393224 | tf_op jit(solution)/shard_map/ppermute | solution.py:428
  26.3 6.5 %collective-permute-start.12 = (bf16[2,16,2048]{2,1,0:T(8,128)(2,1)S(1)}, bf16[2,16,2048]{2,1,0:T(8,128)(2,1)S(1)}, u32[]{:S(2)}, u32[]{:S(2)}) collective-permute-start(bf16[2,16,2048]{2,1,0:T(8,128)(2,1)S(1)} %get-tuple-element.51), channel_id=1, source_target_pairs={{4,0},{8,4},{12,8},{14,12},{10,14},{6,10},{2,6},{0,2},{5,1},{9,5},... | collective-permute-start | bytes 393224 | tf_op jit(solution)/shard_map/ppermute | solution.py:428
  30.2 5.1 %collective-permute-start.10 = (bf16[2,16,2048]{2,1,0:T(8,128)(2,1)S(1)}, bf16[2,16,2048]{2,1,0:T(8,128)(2,1)S(1)}, u32[]{:S(2)}, u32[]{:S(2)}) collective-permute-start(bf16[2,16,2048]{2,1,0:T(8,128)(2,1)S(1)} %collective-permute-done.8.refs_3_), channel_id=1, source_target_pairs={{4,0},{8,4},{12,8},{14,12},{10,14},{6,10},{2,6},{0,2},{5,1},{9,5},... | collective-permute-start | bytes 393224 | tf_op jit(solution)/shard_map/ppermute | solution.py:428
  30.5 5.0 %collective-permute-start.9 = (bf16[2,16,2048]{2,1,0:T(8,128)(2,1)S(1)}, bf16[2,16,2048]{2,1,0:T(8,128)(2,1)S(1)}, u32[]{:S(2)}, u32[]{:S(2)}) collective-permute-start(bf16[2,16,2048]{2,1,0:T(8,128)(2,1)S(1)} %collective-permute-done.7.refs_0_), channel_id=1, source_target_pairs={{0,4},{4,8},{8,12},{12,14},{14,10},{10,6},{6,2},{2,0},{1,5},{5,9},... | collective-permute-start | bytes 393224 | tf_op jit(solution)/shard_map/ppermute | solution.py:428
  35.2 3.1 %copy-start.1 = (f32[2,1024]{1,0:T(2,128)S(1)}, f32[2,1024]{1,0:T(2,128)}, u32[]{:S(2)}) copy-start(f32[2,1024]{1,0:T(2,128)} %filters) | copy-start | bytes 24580
  37.5 1.9 %collective-permute-start.13 = (f32[8,2048]{1,0:T(8,128)S(1)}, f32[8,2048]{1,0:T(8,128)S(1)}, u32[]{:S(2)}, u32[]{:S(2)}) collective-permute-start(f32[8,2048]{1,0:T(8,128)S(1)} %get-tuple-element.58), channel_id=1, source_target_pairs={{0,1},{1,0},{2,3},{3,2},{4,5},{5,4},{6,7},{7,6},{8,9},{9,8},{10,11... | collective-permute-start | bytes 196616 | tf_op jit(solution)/shard_map/ppermute | solution.py:373
where the time goes:
time: 40.7 us; the launch traced here: 40.4 us
  Pallas kernels  19.9 us (49%)
  starting transfers between devices  11.9 us (29%)
  waiting for transfers between devices  7.48 us (18%)
  local copies, waits for them, and re-layouts  1.02 us (3%)
    ppermute x10, starting transfers between devices, step(): return (lax.ppermute(a, 'rx', up), lax.ppermute(b, 'rx', down))  10.9 us
    pallas_call x4, Pallas kernels, add(): call(kernel, [row_shape, row_shape, token], kinds, [pltpu.VMEM((count * s...  9.44 us
    pallas_call x1, Pallas kernels, setup(): call(functools.partial(setup_kernel, own_traces, aper), [struct(spectra_s...  6.63 us
    ppermute x10, waiting for transfers between devices, step(): return (lax.ppermute(a, 'rx', up), lax.ppermute(b, 'rx', down))  6.44 us
    pallas_call x1, Pallas kernels, arrange(): return call(filters_kernel, [struct(filters.shape, F32)], 'v')(filters)[0]  1.07 us
    pallas_call x1, Pallas kernels, per_device(): call(functools.partial(finish_kernel, 1.0 / math.sqrt(aper)), [struct((so...  1.04 us
    ppermute x4, waiting for transfers between devices, swap(): return lax.ppermute(x, 'xl', [(0, 1), (1, 0)])  1.04 us
    ppermute x4, starting transfers between devices, swap(): return lax.ppermute(x, 'xl', [(0, 1), (1, 0)])  1.03 us
  transfers between devices with their start and end apart: 14, of which 7 were waited for; matrix products, arithmetic and copies ran while one was open for 0% of the time, Pallas kernels for 42%

commit v1 on v0

v1 whole, which is shorter than its diff:
```python
import functools
import math

import jax
import jax.numpy as jnp
from jax import lax
from jax.experimental import pallas as pl
from jax.experimental.pallas import tpu as pltpu
from jax.sharding import PartitionSpec as P


F32, BF16, I32 = jnp.float32, jnp.bfloat16, jnp.int32
ROWS = 16
FORWARD_STEP = 32
INVERSE_STEP = 16


def turn(a, b):
    return a[0] * b[0] - a[1] * b[1], a[1] * b[0] + a[0] * b[1]


def angles(multiples, waves, samples):
    phase = ((multiples * waves) & (samples - 1)).astype(F32) * (2.0 * math.pi / samples)
    return jnp.cos(phase), jnp.sin(phase)


def row_of(pair, k):
    return pair[0][k : k + 1], pair[1][k : k + 1]


def build_forward(even, odd, fine):
    count = even.shape[1]
    part = count // 2
    samples = 8 * count
    scale = 1.0 / math.sqrt(samples)
    first, ahead = [], []
    for k, rest in enumerate((0, 2, 1, 5)):
        row = lax.broadcasted_iota(I32, (8, count), 0)
        lane = lax.broadcasted_iota(I32, (8, count), 1)
        wave = 8 * lane + rest
        if k == 0:
            wave = jnp.where(lane < part, 8 * lane, 8 * (lane - part) + 4)
        columns = slice(k * count, (k + 1) * count)
        base = angles(row, wave, samples)
        jumps = angles(jnp.left_shift(8, jnp.minimum(row, 2)), wave, samples)
        base = (base[0] * scale, base[1] * scale)
        fine[0, 0:8, columns], fine[1, 0:8, columns] = base
        more = turn(base, row_of(jumps, 0))
        fine[0, 8:16, columns], fine[1, 8:16, columns] = more
        jump = row_of(jumps, 1)
        fine[0, 16:24, columns], fine[1, 16:24, columns] = turn(base, jump)
        fine[0, 24:32, columns], fine[1, 24:32, columns] = turn(more, jump)
        ahead.append(row_of(jumps, 2))
        first.append((jnp.ones((1, count), F32), jnp.zeros((1, count), F32)))

    def step(i, coarse):
        rows = pl.ds(i * FORWARD_STEP, FORWARD_STEP)
        for k in range(4):
            columns = slice(k * count, (k + 1) * count)
            cosine, sine = turn((fine[0, :, columns], fine[1, :, columns]), coarse[k])
            if k == 0:
                for g in range(2):
                    even[g, rows, :part] = cosine[:, g * part : (g + 1) * part].astype(BF16)
                    even[g, rows, part:] = (-sine[:, g * part : (g + 1) * part]).astype(BF16)
            else:
                odd[k - 1, rows, :count] = cosine.astype(BF16)
                odd[k - 1, rows, count:] = sine.astype(BF16)
        return [turn(a, b) for a, b in zip(coarse, ahead)]

    lax.fori_loop(0, count // FORWARD_STEP, step, first)


def forward_kernel(rx, xl, even, odd, fine):
    build_forward(even, odd, fine)


def inverse_kernel(even, odd, fine):
    count = even.shape[1]
    part = count // 2
    samples = 8 * count
    scale = 1.0 / math.sqrt(samples // 2)
    row = lax.broadcasted_iota(I32, (8, count), 0)
    time = lax.broadcasted_iota(I32, (8, count), 1)
    base = angles(8 * row, time, samples)
    jumps = angles(jnp.where(row == 0, 64, jnp.where(row == 1, 128, row - 1)), time, samples)
    base = (base[0] * scale, base[1] * scale)
    base = (base, turn(base, row_of(jumps, 0)))
    for k, rest in enumerate((0, 4, 2, 1, 5)):
        for half in range(2):
            value = turn(base[half], row_of(jumps, 1 + rest)) if rest else base[half]
            rows = slice(8 * half, 8 * half + 8)
            fine[0, k, rows, :], fine[1, k, rows, :] = value
    ahead = row_of(jumps, 1)
    sign = 1.0 - 2.0 * (time[:1] & 1).astype(F32)

    def step(i, coarse):
        rows = pl.ds(i * INVERSE_STEP, INVERSE_STEP)
        later = pl.ds(part + i * INVERSE_STEP, INVERSE_STEP)
        for k in range(5):
            cosine, sine = turn((fine[0, k], fine[1, k]), coarse)
            if k < 2:
                even[k, rows, :] = cosine.astype(BF16)
                even[k, later, :] = (-sine).astype(BF16)
            else:
                odd[k - 2, rows, :count] = cosine.astype(BF16)
                odd[k - 2, rows, count:] = sine.astype(BF16)
                odd[k - 2, later, :count] = (cosine * sign).astype(BF16)
                odd[k - 2, later, count:] = (sine * sign).astype(BF16)
        return turn(coarse, ahead)

    first = (jnp.ones((1, count), F32), jnp.zeros((1, count), F32))
    lax.fori_loop(0, part // INVERSE_STEP, step, first)


def filters_kernel(filters, out):
    count = filters.shape[1]
    part = count // 8
    column = lax.broadcasted_iota(I32, (count, count), 1)
    block, inner = column // part, column % part
    rest = jnp.zeros_like(column)
    for k, value in enumerate((0, 4, 2, 6, 1, 7, 5, 3)):
        rest = jnp.where(block == k, value, rest)
    upper = ((block == 3) | (block == 5) | (block == 7)).astype(I32)
    source = 8 * jnp.where(upper == 1, part - 1 - inner, inner) + rest
    move = (lax.broadcasted_iota(I32, (count, count), 0) == source).astype(F32).astype(BF16)
    left = filters[...]
    moved = jnp.zeros((2, count), F32)
    for _ in range(3):
        piece = left.astype(BF16)
        left = left - piece.astype(F32)
        moved = moved + jnp.dot(piece, move, preferred_element_type=F32)
    out[0:1, :] = moved[0:1]
    out[1:2, :] = jnp.where(upper[:1] == 1, -moved[1:2], moved[1:2])


def split(x):
    quarter = x.shape[-1] // 4
    half = quarter // 2
    x0, x1, x2, x3 = (x[:, q * quarter : (q + 1) * quarter].astype(F32) for q in range(4))
    first, second = x0 + x2, x1 + x3
    p, q = first + second, first - second
    re, im = x0 - x2, x3 - x1
    root = math.sqrt(0.5)
    turned_re = root * (re[:, half:] + im[:, half:])
    turned_im = root * (im[:, half:] - re[:, half:])
    re, im = re[:, :half], im[:, :half]
    return (
        (p[:, :half] + p[:, half:]).astype(BF16),
        (p[:, :half] - p[:, half:]).astype(BF16),
        (q[:, :half].astype(BF16), (-q[:, half:]).astype(BF16)),
        ((re + turned_re).astype(BF16), (im + turned_im).astype(BF16)),
        ((re - turned_re).astype(BF16), (im - turned_im).astype(BF16)),
    )


def transform(parts, even, odd):
    rows = parts[0].shape[0]
    count = even.shape[1]
    dot = functools.partial(jnp.dot, preferred_element_type=F32)
    for g in range(2):
        yield dot(parts[g], even[g])
    for g in range(3):
        both = dot(jnp.concatenate(parts[2 + g], axis=0), odd[g])
        yield both[:rows, :count] + both[rows:, count:]
        yield both[rows:, :count] - both[:rows, count:]


def groups(samples):
    count = samples // 8
    part = count // 2
    full = [(2 * count + 2 * g * count, count, count) for g in range(3)]
    return [(0, part, part), (count, part, part), *full]


def setup_kernel(per_device, aper, place, own, other, notes, notes_other, even, odd, out, token, data, arriving):
    rec_dev, samples = own.shape
    copies = [
        pltpu.make_async_copy(source, data.at[k * rec_dev : (k + 1) * rec_dev], arriving.at[k])
        for k, source in enumerate((own, other))
    ]
    for copy in copies:
        copy.start()
    core = place[0]
    slots = 2 * rec_dev
    outs = slots // aper
    out_dev = outs // 2
    earlier = (
        lax.broadcasted_iota(I32, (rec_dev, rec_dev), 0)
        < lax.broadcasted_iota(I32, (rec_dev, rec_dev), 1)
    ).astype(F32).astype(BF16)
    lines = rec_dev // aper
    sides = [
        jnp.concatenate([note[k : k + 1, :] for k in range(lines)], axis=1)
        for note in (notes, notes_other)
    ]
    ranks, totals = [], []
    for owner in sides:
        mine = (owner == core).astype(F32)
        rank = jnp.dot(
            jnp.broadcast_to(mine, (8, rec_dev)).astype(BF16), earlier, preferred_element_type=F32
        )
        ranks.append(rank[:1])
        totals.append(jnp.sum(mine, axis=1, keepdims=True))
    position = lax.broadcasted_iota(I32, (1, rec_dev), 1)
    slot_row = lax.broadcasted_iota(I32, (slots, rec_dev), 0)
    picks = []
    for side in range(2):
        second = core != side
        before = (ranks[side] + jnp.where(second, totals[1 - side], 0.0)).astype(I32)
        index = position + jnp.where(second, rec_dev, 0)
        slot = jnp.where(sides[side] == core, before, rec_dev + index - before)
        picks.append((slot_row == slot).astype(F32).astype(BF16))
    picks = jnp.concatenate(picks, axis=1)
    trace = lax.broadcasted_iota(I32, (aper, aper), 0)
    trace = trace // per_device * (2 * per_device) + core * per_device + trace % per_device
    rows = []
    for r in range(outs):
        line = lines + r % out_dev
        entry = (notes if r < out_dev else notes_other)[line : line + 1, :]
        match = (trace == entry).astype(F32).astype(BF16)
        pick = picks[r * aper : (r + 1) * aper]
        rows.append(jnp.dot(match, pick, preferred_element_type=F32).astype(BF16))
    placed = jnp.concatenate(rows, axis=0)
    for copy in copies:
        copy.wait()
    routed = jnp.dot(placed, data[...], preferred_element_type=F32)
    first = 0
    for block in transform(split(routed), even, odd):
        width = block.shape[1]
        block = block.astype(BF16).reshape(outs, aper // ROWS, ROWS, width)
        for r in range(outs):
            out[:, r, :, first : first + width] = block[r]
        first += width
    token[...] = jnp.zeros(token.shape, F32)


def ring_chunk(me, offset):
    place = jnp.where(me % 2 == 0, me // 2, 7 - me // 2)
    place = (place + offset) % 8
    return jnp.where(place < 4, 2 * place, 15 - 2 * place)


def sum_rows(values):
    row = lax.broadcasted_iota(I32, values[0].shape, 0)
    for shift in (4, 2, 1):
        upper = row % (2 * shift) < shift
        half = len(values) // 2
        joined = []
        for a, b in zip(values[:half], values[half:]):
            if shift == 4:
                rolled = pltpu.roll(jnp.where(upper, b, a), 4, 0)
            else:
                rolled = jnp.where(upper, pltpu.roll(a, 8 - shift, 0), pltpu.roll(b, shift, 0))
            joined.append(jnp.where(upper, a, b) + rolled)
        values = joined
    return values[0]


def halves_kernel(*refs):
    values, outs = refs[: len(refs) // 3], refs[len(refs) // 3 :]
    cut = outs[0].shape[0]
    for k, value in enumerate(values):
        outs[2 * k][...] = value[:cut]
        outs[2 * k + 1][...] = value[cut:]


def products_kernel(offsets, count, ringed, with_total, extra, place, *refs):
    pieces = refs[:count]
    even, odd, spectra = refs[count : count + 3]
    totals = refs[count + 3 : count + 3 + 2 * with_total]
    outs = refs[count + 3 + 2 * with_total + extra : -1]
    work = refs[-1]
    chunks = [ring_chunk(place[0], offset) if ringed else offset for offset in offsets]
    samples = work.shape[1]
    number = spectra.shape[1]
    rows = work.shape[0] // len(offsets)
    sources = rows // ROWS
    data = jnp.concatenate([x[...].reshape(-1, samples) for x in pieces], axis=0)
    first = 0
    for block in transform(split(data), even, odd):
        work[:, first : first + block.shape[1]] = block
        first += block.shape[1]
    if len(outs) > 2:
        outs[2][...] = jnp.zeros(outs[2].shape, F32)
    for start, distance, width in groups(samples):
        for block in range(width // 128):
            re = pl.ds(start + block * 128, 128)
            im = pl.ds(start + distance + block * 128, 128)
            sums = {}
            for c in range(len(offsets)):
                for r in range(number):
                    right = [spectra[chunks[c], r, :, k].astype(F32) for k in (re, im)]
                    for h in range(ROWS // 8):
                        b_re, b_im = (b[8 * h : 8 * h + 8] for b in right)
                        for s in range(sources):
                            top = c * rows + s * ROWS + h * 8
                            a_re, a_im = work[top : top + 8, re], work[top : top + 8, im]
                            x = a_re * b_re - a_im * b_im
                            y = a_re * b_im + a_im * b_re
                            if (s, r) in sums:
                                x, y = x + sums[s, r][0], y + sums[s, r][1]
                            sums[s, r] = (x, y)
            share = number // 2
            for i in range(2):
                keys = [(s, i * share + r) for r in range(share) for s in range(sources)]
                for part, columns in enumerate((re, im)):
                    value = sum_rows([sums[key][part] for key in keys])
                    if with_total:
                        value = value + totals[i][:, columns]
                    outs[i][:, columns] = value


def finish_kernel(scale, filters, mine, arrived, even, odd, out):
    count = even.shape[1]
    sources, out_dev, samples = out.shape
    raw = mine[...] + arrived[...]
    rows = raw.shape[0]
    dot = functools.partial(jnp.dot, preferred_element_type=F32)
    waves, column = [], 0
    for g, (start, distance, width) in enumerate(groups(samples)):
        g_re = filters[0:1, column : column + width] * scale
        g_im = filters[1:2, column : column + width] * scale
        column += width
        x = raw[:, start : start + width]
        y = raw[:, start + distance : start + distance + width]
        x, y = g_re * x - g_im * y, g_re * y + g_im * x
        if g < 2:
            waves.append(dot(jnp.concatenate([x, y], axis=1).astype(BF16), even[g]))
        else:
            both = dot(jnp.concatenate([x, y], axis=0).astype(BF16), odd[g - 2])
            waves.append(both[:rows, :count] - both[rows:, count:])
            waves.append(both[:rows, count:] + both[rows:, :count])
    a, b, h_re, h_im, v_re, v_im, w_re, w_im = waves
    root = math.sqrt(0.5)
    plus, minus = a + b, a - b
    u_re, u_im = v_re + w_re, v_im + w_im
    v_re, v_im = v_re - w_re, v_im - w_im
    less, more = root * (v_re - v_im), root * (v_re + v_im)
    results = (
        plus + h_re + u_re,
        minus - h_im + less,
        plus - h_re - u_im,
        minus + h_im - more,
        plus + h_re - u_re,
        minus - h_im - less,
        plus - h_re + u_im,
        minus + h_im + more,
    )
    for k, value in enumerate(results):
        value = value.reshape(out_dev, sources, count)
        for r in range(out_dev):
            out[:, r, k * count : (k + 1) * count] = value[r].astype(BF16)


def call(kernel, out_shape, kinds, scratch=(), limit=24, cost=1):
    spaces = {"s": pltpu.SMEM, "v": pltpu.VMEM, "a": pl.ANY}
    specs = [pl.BlockSpec(memory_space=spaces[k]) for k in kinds]
    return pl.pallas_call(
        kernel,
        out_shape=out_shape,
        in_specs=specs,
        out_specs=[pl.BlockSpec(memory_space=pltpu.VMEM)] * len(out_shape),
        cost_estimate=pl.CostEstimate(
            flops=cost * 10**9, transcendentals=0, bytes_accessed=cost * 3 * 10**6
        ),
        scratch_shapes=list(scratch),
        compiler_params=pltpu.CompilerParams(vmem_limit_bytes=limit << 20),
    )


def per_device(ring_size, source_traces, surface_filter, records, owners, aperture):
    sources, own_traces, samples = source_traces.shape
    out_dev, aper = aperture.shape
    rec_dev = records.shape[0]
    count = samples // 8
    struct = jax.ShapeDtypeStruct
    rx, xl = (lax.axis_index(axis).astype(I32).reshape(1) for axis in ("rx", "xl"))
    outs = 2 * out_dev
    chunks = aper // ROWS
    token = struct((8, 128), F32)

    def after(token, *values):
        return lax.optimization_barrier((*values, token))

    def swap(x):
        return lax.ppermute(x, "xl", [(0, 1), (1, 0)])

    notes = jnp.concatenate([owners.reshape(-1, aper), aperture], axis=0)
    table_shapes = [struct((2, count, count), BF16), struct((3, count, 2 * count), BF16)]
    fine = [pltpu.VMEM((2, FORWARD_STEP, 4 * count), F32)]
    tables = call(forward_kernel, table_shapes, "ss", fine)(rx, xl)

    def setup():
        return call(
            functools.partial(setup_kernel, own_traces, aper),
            [struct((chunks, outs, ROWS, samples), BF16), token],
            "saavvvv",
            [pltpu.VMEM((2 * rec_dev, samples), BF16), pltpu.SemaphoreType.DMA((2,))],
            cost=4,
        )(xl, records, swap(records), notes, swap(notes), *tables)

    def arrange(filters):
        return call(filters_kernel, [struct(filters.shape, F32)], "v")(filters)[0]

    def add(pieces, offsets, totals, ringed, extra=()):
        kernel = functools.partial(
            products_kernel, offsets, len(pieces), ringed, bool(totals), len(extra)
        )
        arguments = [*pieces, *tables, spectra, *totals, *extra]
        row_shape = struct((out_dev * sources, samples), F32)
        kinds = "s" + "v" * len(arguments)
        *result, done = call(
            kernel,
            [row_shape, row_shape, token],
            kinds,
            [pltpu.VMEM((len(offsets) * sources * ROWS, samples), F32)],
        )(rx, *arguments)
        return result, done

    if ring_size == 8 and own_traces == ROWS:
        order = [0, 2, 4, 6, 7, 5, 3, 1]
        up = [(order[i], order[(i + 1) % 8]) for i in range(8)]
        down = [(b, a) for a, b in up]

        def rise(x):
            return lax.ppermute(x, "rx", up)

        def fall(x):
            return lax.ppermute(x, "rx", down)

        half = struct((sources // 2, own_traces, samples), BF16)

        def halves(x):
            return call(halves_kernel, [half] * 2, "v")(x)

        a1, b1 = rise(source_traces), fall(source_traces)
        spectra, done = setup()
        a2, first = after(done, a1)
        b2, second = after(done, b1)
        a2, b2 = rise(a2), fall(b2)
        totals, done = add([source_traces, a1, b1], [0, -1, 1], [], True, [first, second])
        filters = arrange(surface_filter)
        a3, filters, first = after(done, a2, filters)
        b3, second = after(done, b2)
        a3_sent, a3_kept = halves(a3)
        b3_kept, b3_sent = halves(b3)
        a3_sent, b3_sent = rise(a3_sent), fall(b3_sent)
        a3_kept, b3_kept = rise(a3_kept), fall(b3_kept)
        totals, done = add([a2, b2], [-2, 2], totals, True, [first, second])
        a4, first = after(done, a3_sent)
        b4, second = after(done, b3_sent)
        a4, b4 = rise(a4), fall(b4)
        pieces = [a3_sent, a3_kept, b3_kept, b3_sent]
        totals, _ = add(pieces, [-3, 3], totals, True, [first, second])
        (mine, theirs), _ = add([a4, b4], [4], totals, True)
    else:
        spectra, _ = setup()
        gathered = lax.all_gather(source_traces, "rx", axis=1, tiled=True)
        parts = [gathered[:, k * ROWS : (k + 1) * ROWS] for k in range(chunks)]
        totals = []
        for k in range(0, chunks, 2):
            totals, _ = add(parts[k : k + 2], [k, k + 1], totals, False)
        mine, theirs = totals
        filters = arrange(surface_filter)

    fine = [pltpu.VMEM((2, 5, INVERSE_STEP, count), F32)]
    inverse = call(inverse_kernel, table_shapes, "", fine)()
    return call(
        functools.partial(finish_kernel, 1.0 / math.sqrt(aper)),
        [struct((sources, out_dev, samples), BF16)],
        "vvvvv",
    )(filters, mine, swap(theirs), *inverse)[0]


def solution(mesh):
    in_specs = (
        P(None, ("groups", "rx", "xl"), None),
        P(),
        P(("groups", "rx", "xl"), None),
        P(("groups", "rx", "xl")),
        P(("groups", "rx", "xl"), None),
    )
    out_specs = P(None, ("groups", "rx", "xl"), None)
    return jax.shard_map(
        functools.partial(per_device, mesh.shape["rx"]),
        mesh=mesh,
        in_specs=in_specs,
        out_specs=out_specs,
        check_vma=False,
    )
```

time: 40.7 us -> 35.3 us (0.87)
  Pallas kernels: 19.9 us -> 11.7 us
  waiting for transfers between devices: 7.48 us -> 11.2 us
  local copies, waits for them, and re-layouts: 1.02 us -> 0.01 us
  other arithmetic: 0 us -> 0.7 us
    pallas_call x8 -> x9, Pallas kernels: 17.8 us -> 9.61 us  [the longest x4 5.52 us: add(): call(kernel, [row_shape, row_shape, token], kinds, [pltpu.VMEM((len(offse...]
    ppermute x10, waiting for transfers between devices: 6.44 us -> 9.96 us  [the longest x5 7.34 us: fall(): return lax.ppermute(x, 'rx', down)]
    unnamed x10 -> x6, local copies, waits for them, and re-layouts: 1.02 us -> 0.01 us
    concatenate x0 -> x1, other arithmetic: none -> 0.7 us  [per_device(): notes = jnp.concatenate([owners.reshape(-1, aper), aperture], axis=0)]
    ppermute x4 -> x3, starting transfers between devices: 1.03 us -> 0.6 us  [swap(): return lax.ppermute(x, 'xl', [(0, 1), (1, 0)])]
    ppermute x4 -> x3, waiting for transfers between devices: 1.04 us -> 1.28 us  [swap(): return lax.ppermute(x, 'xl', [(0, 1), (1, 0)])]
  transfers between devices with their start and end apart: 14 -> 13, of which waited for: 7 -> 9; matrix products, arithmetic and copies ran while one was open for 0% -> 2% of each run, Pallas kernels for 42% -> 27%
where the time goes in v1:
time: 35.3 us; the launch traced here: 35.2 us
  Pallas kernels  11.7 us (33%)
  starting transfers between devices  11.5 us (33%)
  waiting for transfers between devices  11.2 us (32%)
  other arithmetic  0.7 us (2%)
    ppermute x5, starting transfers between devices, fall(): return lax.ppermute(x, 'rx', down)  8.73 us
    ppermute x5, waiting for transfers between devices, fall(): return lax.ppermute(x, 'rx', down)  7.34 us
    pallas_call x4, Pallas kernels, add(): call(kernel, [row_shape, row_shape, token], kinds, [pltpu.VMEM((len(offse...  5.52 us
    pallas_call x1, Pallas kernels, setup(): call(functools.partial(setup_kernel, own_traces, aper), [struct((chunks,...  3.09 us
    ppermute x5, waiting for transfers between devices, rise(): return lax.ppermute(x, 'rx', up)  2.62 us
    ppermute x5, starting transfers between devices, rise(): return lax.ppermute(x, 'rx', up)  2.16 us
    ppermute x3, waiting for transfers between devices, swap(): return lax.ppermute(x, 'xl', [(0, 1), (1, 0)])  1.28 us
    pallas_call x1, Pallas kernels, arrange(): return call(filters_kernel, [struct(filters.shape, F32)], 'v')(filters)[0]  1.12 us
  transfers between devices with their start and end apart: 13, of which 9 were waited for; matrix products, arithmetic and copies ran while one was open for 2% of the time, Pallas kernels for 27%

profile of v1, /device:TPU:0, one launch (start us, length us, event | category | flops | bytes accessed | tf_op | source)
XLA Modules:
  0.0 35.2 jit_solution(18053288243359037231)
XLA Ops:
  0.0 0.0 copy-start.1
  0.0 0.5 %collective-permute-start.1 = (bf16[256,2048]{1,0:T(8,128)(2,1)}, bf16[256,2048]{1,0:T(8,128)(2,1)S(1)}, u32[]{:S(2)}, u32[]{:S(2)}) collective-permute-start(bf16[256,2048]{1,0:T(8,128)(2,1)} %own.1), channel_id=1, source_target_pairs={{0,1},{1,0},{2,3},{3,2},{4,5},{5,4},{6,7},{7,6},{8,9},{9,8},{10,11... | collective-permute-start | bytes 3145736 | tf_op jit(solution)/shard_map/ppermute | solution.py:386
  0.5 2.5 %collective-permute-start.4 = (bf16[4,16,2048]{2,1,0:T(8,128)(2,1)}, bf16[4,16,2048]{2,1,0:T(8,128)(2,1)S(1)}, u32[]{:S(2)}, u32[]{:S(2)}) collective-permute-start(bf16[4,16,2048]{2,1,0:T(8,128)(2,1)} %refs_0_.1), channel_id=1, source_target_pairs={{4,0},{8,4},{12,8},{14,12},{10,14},{6,10},{2,6},{0,2},{5,1},{9,5},... | collective-permute-start | bytes 786440 | tf_op jit(solution)/shard_map/ppermute | solution.py:429
  3.0 0.2 collective-permute-start
  3.1 0.7 %pad_add_fusion.notes = s32[4,128]{1,0:T(4,128)S(1)} fusion(s32[2,128]{1,0:T(2,128)} %param.9, s32[2,128]{1,0:T(2,128)} %bitcast.3), kind=kLoop, calls=%fused_computation | loop fusion | flops 512 | bytes 4096 | tf_op jit(solution)/shard_map/concatenate | solution.py:388
  3.8 0.1 collective-permute-start.2
  4.0 0.6 %shard_map.55 = (bf16[2,256,256]{2,1,0:T(8,128)(2,1)S(1)}, bf16[3,256,512]{2,1,0:T(8,128)(2,1)S(1)}) custom-call(s32[1]{0:T(128)} %bitcast.2.rx.place, s32[1]{0:T(128)} %bitcast.xl.place), custom_call_target="tpu_custom_call" | custom-call | flops 1000000000 | bytes 3000000 | tf_op jit(solution)/shard_map/pallas_call | solution.py:391
  4.6 0.4 %collective-permute-done.2.notes_other = s32[4,128]{1,0:T(4,128)S(1)} collective-permute-done((s32[4,128]{1,0:T(4,128)S(1)}, s32[4,128]{1,0:T(4,128)S(1)}, u32[]{:S(2)}, u32[]{:S(2)}) %collective-permute-start.2) | collective-permute-done | bytes 2080 | tf_op jit(solution)/shard_map/ppermute | solution.py:386
  5.0 0.0 collective-permute-done.1.other
  5.0 0.0 copy-done.1
  5.0 0.0 copy-start.2
  5.0 3.1 %shard_map.56 = (bf16[8,4,16,2048]{3,2,1,0:T(8,128)(2,1)S(1)}, f32[8,128]{1,0:T(8,128)S(1)}) custom-call(s32[1]{0:T(128)} %bitcast.xl.place, bf16[256,2048]{1,0:T(8,128)(2,1)S(1)} %copy-done.1, bf16[256,2048]{1,0:T(8,128)(2,1)S(1)} %collective-permute-done.1.other, s32[4,128]{1,0:T(4,128)S(1)} %pad_add_fusion.notes, ...), custom_call_target="tpu_custom_call" | custom-call | flops 4000000000 | bytes 12000000 | tf_op jit(solution)/shard_map/pallas_call | solution.py:394
  8.1 0.0 copy-start
  8.1 2.1 %collective-permute-done.4.refs_2_ = bf16[4,16,2048]{2,1,0:T(8,128)(2,1)S(1)} collective-permute-done((bf16[4,16,2048]{2,1,0:T(8,128)(2,1)}, bf16[4,16,2048]{2,1,0:T(8,128)(2,1)S(1)}, u32[]{:S(2)}, u32[]{:S(2)}) %collective-permute-start.4) | collective-permute-done | bytes 262176 | tf_op jit(solution)/shard_map/ppermute | solution.py:429
  10.2 1.7 %collective-permute-start.6 = (bf16[4,16,2048]{2,1,0:T(8,128)(2,1)S(1)}, bf16[4,16,2048]{2,1,0:T(8,128)(2,1)S(1)}, u32[]{:S(2)}, u32[]{:S(2)}) collective-permute-start(bf16[4,16,2048]{2,1,0:T(8,128)(2,1)S(1)} %collective-permute-done.4.refs_2_), channel_id=1, source_target_pairs={{4,0},{8,4},{12,8},{14,12},{10,14},{6,10},{2,6},{0,2},{5,1},{9,5},... | collective-permute-start | bytes 786440 | tf_op jit(solution)/shard_map/ppermute | solution.py:429
  11.9 0.0 collective-permute-done.refs_1_
  11.9 0.4 %collective-permute-start.3 = (bf16[4,16,2048]{2,1,0:T(8,128)(2,1)S(1)}, bf16[4,16,2048]{2,1,0:T(8,128)(2,1)S(1)}, u32[]{:S(2)}, u32[]{:S(2)}) collective-permute-start(bf16[4,16,2048]{2,1,0:T(8,128)(2,1)S(1)} %collective-permute-done.refs_1_), channel_id=1, source_target_pairs={{0,4},{4,8},{8,12},{12,14},{14,10},{10,6},{6,2},{2,0},{1,5},{5,9},... | collective-permute-start | bytes 786440 | tf_op jit(solution)/shard_map/ppermute | solution.py:426
  12.2 0.0 copy-done.2
  12.2 1.1 %shard_map.57.filters = f32[2,1024]{1,0:T(2,128)S(1)} custom-call(f32[2,1024]{1,0:T(2,128)S(1)} %copy-done.2), custom_call_target="tpu_custom_call" | custom-call | flops 1000000000 | bytes 3000000 | tf_op jit(solution)/shard_map/pallas_call | solution.py:403
  13.4 0.0 copy-done
  13.4 1.6 %shard_map.58 = (f32[8,2048]{1,0:T(8,128)S(1)}, f32[8,2048]{1,0:T(8,128)S(1)}, f32[8,128]{1,0:T(8,128)S(1)}) custom-call(s32[1]{0:T(128)} %bitcast.2.rx.place, bf16[4,16,2048]{2,1,0:T(8,128)(2,1)S(1)} %copy-done, bf16[4,16,2048]{2,1,0:T(8,128)(2,1)S(1)} %collective-permute-done.refs_1_, bf16[4,16,2048]{2,1,0:T(8,128)(2,1)S(1)} %collective-permute-done.4.refs_2_, ...), custom_call_target="tpu_custom_call" | custom-call | flops 1000000000 | bytes 3000000 | tf_op jit(solution)/shard_map/pallas_call | solution.py:412
  15.0 3.3 %collective-permute-done.6.refs_1_.refs_0_ = bf16[4,16,2048]{2,1,0:T(8,128)(2,1)S(1)} collective-permute-done((bf16[4,16,2048]{2,1,0:T(8,128)(2,1)S(1)}, bf16[4,16,2048]{2,1,0:T(8,128)(2,1)S(1)}, u32[]{:S(2)}, u32[]{:S(2)}) %collective-permute-start.6) | collective-permute-done | bytes 262176 | tf_op jit(solution)/shard_map/ppermute | solution.py:429
  18.3 1.5 %collective-permute-start.8 = (bf16[2,16,2048]{2,1,0:T(8,128)(2,1)S(1)}, bf16[2,16,2048]{2,1,0:T(8,128)(2,1)S(1)}, u32[]{:S(2)}, u32[]{:S(2)}) collective-permute-start(bf16[2,16,2048]{2,1,0:T(8,128)(2,1)S(1)} %get-tuple-element.57), channel_id=1, source_target_pairs={{4,0},{8,4},{12,8},{14,12},{10,14},{6,10},{2,6},{0,2},{5,1},{9,5},... | collective-permute-start | bytes 393224 | tf_op jit(solution)/shard_map/ppermute | solution.py:429
  19.8 0.0 collective-permute-done.3.refs_0_
  19.9 0.6 %collective-permute-start.5 = (bf16[2,16,2048]{2,1,0:T(8,128)(2,1)S(1)}, bf16[2,16,2048]{2,1,0:T(8,128)(2,1)S(1)}, u32[]{:S(2)}, u32[]{:S(2)}) collective-permute-start(bf16[2,16,2048]{2,1,0:T(8,128)(2,1)S(1)} %get-tuple-element.48), channel_id=1, source_target_pairs={{0,4},{4,8},{8,12},{12,14},{14,10},{10,6},{6,2},{2,0},{1,5},{5,9},... | collective-permute-start | bytes 393224 | tf_op jit(solution)/shard_map/ppermute | solution.py:426
  20.5 1.5 %collective-permute-start.11 = (bf16[2,16,2048]{2,1,0:T(8,128)(2,1)S(1)}, bf16[2,16,2048]{2,1,0:T(8,128)(2,1)S(1)}, u32[]{:S(2)}, u32[]{:S(2)}) collective-permute-start(bf16[2,16,2048]{2,1,0:T(8,128)(2,1)S(1)} %get-tuple-element.60), channel_id=1, source_target_pairs={{4,0},{8,4},{12,8},{14,12},{10,14},{6,10},{2,6},{0,2},{5,1},{9,5},... | collective-permute-start | bytes 393224 | tf_op jit(solution)/shard_map/ppermute | solution.py:429
  21.9 0.6 %collective-permute-start.10 = (bf16[2,16,2048]{2,1,0:T(8,128)(2,1)S(1)}, bf16[2,16,2048]{2,1,0:T(8,128)(2,1)S(1)}, u32[]{:S(2)}, u32[]{:S(2)}) collective-permute-start(bf16[2,16,2048]{2,1,0:T(8,128)(2,1)S(1)} %get-tuple-element.59), channel_id=1, source_target_pairs={{0,4},{4,8},{8,12},{12,14},{14,10},{10,6},{6,2},{2,0},{1,5},{5,9},... | collective-permute-start | bytes 393224 | tf_op jit(solution)/shard_map/ppermute | solution.py:426
  22.5 1.1 %shard_map.60 = (f32[8,2048]{1,0:T(8,128)S(1)}, f32[8,2048]{1,0:T(8,128)S(1)}, f32[8,128]{1,0:T(8,128)S(1)}) custom-call(s32[1]{0:T(128)} %bitcast.2.rx.place, bf16[4,16,2048]{2,1,0:T(8,128)(2,1)S(1)} %collective-permute-done.3.refs_0_, bf16[4,16,2048]{2,1,0:T(8,128)(2,1)S(1)} %collective-permute-done.6.refs_1_.refs_0_, ...), custom_call_target="tpu_custom_call" | custom-call | flops 1000000000 | bytes 3000000 | tf_op jit(solution)/shard_map/pallas_call | solution.py:412
  23.6 0.8 %collective-permute-done.8.refs_3_ = bf16[2,16,2048]{2,1,0:T(8,128)(2,1)S(1)} collective-permute-done((bf16[2,16,2048]{2,1,0:T(8,128)(2,1)S(1)}, bf16[2,16,2048]{2,1,0:T(8,128)(2,1)S(1)}, u32[]{:S(2)}, u32[]{:S(2)}) %collective-permute-start.8) | collective-permute-done | bytes 131104 | tf_op jit(solution)/shard_map/ppermute | solution.py:429
  24.3 0.9 %collective-permute-done.5.refs_0_ = bf16[2,16,2048]{2,1,0:T(8,128)(2,1)S(1)} collective-permute-done((bf16[2,16,2048]{2,1,0:T(8,128)(2,1)S(1)}, bf16[2,16,2048]{2,1,0:T(8,128)(2,1)S(1)}, u32[]{:S(2)}, u32[]{:S(2)}) %collective-permute-start.5) | collective-permute-done | bytes 131104 | tf_op jit(solution)/shard_map/ppermute | solution.py:426
  25.3 1.6 %collective-permute-start.9 = (bf16[2,16,2048]{2,1,0:T(8,128)(2,1)S(1)}, bf16[2,16,2048]{2,1,0:T(8,128)(2,1)S(1)}, u32[]{:S(2)}, u32[]{:S(2)}) collective-permute-start(bf16[2,16,2048]{2,1,0:T(8,128)(2,1)S(1)} %collective-permute-done.8.refs_3_), channel_id=1, source_target_pairs={{4,0},{8,4},{12,8},{14,12},{10,14},{6,10},{2,6},{0,2},{5,1},{9,5},... | collective-permute-start | bytes 393224 | tf_op jit(solution)/shard_map/ppermute | solution.py:429
  26.9 0.4 %collective-permute-start.7 = (bf16[2,16,2048]{2,1,0:T(8,128)(2,1)S(1)}, bf16[2,16,2048]{2,1,0:T(8,128)(2,1)S(1)}, u32[]{:S(2)}, u32[]{:S(2)}) collective-permute-start(bf16[2,16,2048]{2,1,0:T(8,128)(2,1)S(1)} %collective-permute-done.5.refs_0_), channel_id=1, source_target_pairs={{0,4},{4,8},{8,12},{12,14},{14,10},{10,6},{6,2},{2,0},{1,5},{5,9},... | collective-permute-start | bytes 393224 | tf_op jit(solution)/shard_map/ppermute | solution.py:426
  27.3 0.0 collective-permute-done.11.refs_2_
  27.3 0.1 collective-permute-done.10.refs_1_
  27.4 1.7 %shard_map.62 = (f32[8,2048]{1,0:T(8,128)S(1)}, f32[8,2048]{1,0:T(8,128)S(1)}, f32[8,128]{1,0:T(8,128)}) custom-call(s32[1]{0:T(128)} %bitcast.2.rx.place, bf16[2,16,2048]{2,1,0:T(8,128)(2,1)S(1)} %collective-permute-done.5.refs_0_, bf16[2,16,2048]{2,1,0:T(8,128)(2,1)S(1)} %collective-permute-done.10.refs_1_, ...), custom_call_target="tpu_custom_call" | custom-call | flops 1000000000 | bytes 3000000 | tf_op jit(solution)/shard_map/pallas_call | solution.py:412
  29.1 1.2 %collective-permute-done.9.refs_1_ = bf16[2,16,2048]{2,1,0:T(8,128)(2,1)S(1)} collective-permute-done((bf16[2,16,2048]{2,1,0:T(8,128)(2,1)S(1)}, bf16[2,16,2048]{2,1,0:T(8,128)(2,1)S(1)}, u32[]{:S(2)}, u32[]{:S(2)}) %collective-permute-start.9) | collective-permute-done | bytes 131104 | tf_op jit(solution)/shard_map/ppermute | solution.py:429
  30.3 1.6 %collective-permute-done.7.refs_0_ = bf16[2,16,2048]{2,1,0:T(8,128)(2,1)S(1)} collective-permute-done((bf16[2,16,2048]{2,1,0:T(8,128)(2,1)S(1)}, bf16[2,16,2048]{2,1,0:T(8,128)(2,1)S(1)}, u32[]{:S(2)}, u32[]{:S(2)}) %collective-permute-start.7) | collective-permute-done | bytes 131104 | tf_op jit(solution)/shard_map/ppermute | solution.py:426
  31.8 1.2 %shard_map.63 = (f32[8,2048]{1,0:T(8,128)S(1)}, f32[8,2048]{1,0:T(8,128)S(1)}, f32[8,128]{1,0:T(8,128)}) custom-call(s32[1]{0:T(128)} %bitcast.2.rx.place, bf16[2,16,2048]{2,1,0:T(8,128)(2,1)S(1)} %collective-permute-done.7.refs_0_, bf16[2,16,2048]{2,1,0:T(8,128)(2,1)S(1)} %collective-permute-done.9.refs_1_, ...), custom_call_target="tpu_custom_call" | custom-call | flops 1000000000 | bytes 3000000 | tf_op jit(solution)/shard_map/pallas_call | solution.py:412
  33.0 0.0 collective-permute-start.12
  33.0 0.3 shard_map.64
  33.4 0.9 %collective-permute-done.12.arrived = f32[8,2048]{1,0:T(8,128)S(1)} collective-permute-done((f32[8,2048]{1,0:T(8,128)S(1)}, f32[8,2048]{1,0:T(8,128)S(1)}, u32[]{:S(2)}, u32[]{:S(2)}) %collective-permute-start.12) | collective-permute-done | bytes 65568 | tf_op jit(solution)/shard_map/ppermute | solution.py:386
  34.3 0.9 %shard_map.65 = bf16[4,2,2048]{2,1,0:T(2,128)(2,1)} custom-call(f32[2,1024]{1,0:T(2,128)S(1)} %shard_map.57.filters, f32[8,2048]{1,0:T(8,128)S(1)} %get-tuple-element.67.mine, f32[8,2048]{1,0:T(8,128)S(1)} %collective-permute-done.12.arrived, bf16[2,256,256]{2,1,0:T(8,128)(2,1)S(1)} %get-tuple-element.69.even, bf16[3,256,512]{2,1,0:T(8,128)(2,1)S(1)} %get-tuple-element.70.odd), custom_call_target="tpu_custom_call" | custom-call | flops 1000000000 | bytes 3000000 | tf_op jit(solution)/shard_map/pallas_call | solution.py:468
  (2 shorter events, 0.0 us)
Async XLA Ops:
  0.0 5.0 %copy-start.1 = (bf16[256,2048]{1,0:T(8,128)(2,1)S(1)}, bf16[256,2048]{1,0:T(8,128)(2,1)}, u32[]{:S(2)}) copy-start(bf16[256,2048]{1,0:T(8,128)(2,1)} %own.1) | copy-start | bytes 3145732
  0.0 5.0 %collective-permute-start.1 = (bf16[256,2048]{1,0:T(8,128)(2,1)}, bf16[256,2048]{1,0:T(8,128)(2,1)S(1)}, u32[]{:S(2)}, u32[]{:S(2)}) collective-permute-start(bf16[256,2048]{1,0:T(8,128)(2,1)} %own.1), channel_id=1, source_target_pairs={{0,1},{1,0},{2,3},{3,2},{4,5},{5,4},{6,7},{7,6},{8,9},{9,8},{10,11... | collective-permute-start | bytes 3145736 | tf_op jit(solution)/shard_map/ppermute | solution.py:386
  0.5 9.8 %collective-permute-start.4 = (bf16[4,16,2048]{2,1,0:T(8,128)(2,1)}, bf16[4,16,2048]{2,1,0:T(8,128)(2,1)S(1)}, u32[]{:S(2)}, u32[]{:S(2)}) collective-permute-start(bf16[4,16,2048]{2,1,0:T(8,128)(2,1)} %refs_0_.1), channel_id=1, source_target_pairs={{4,0},{8,4},{12,8},{14,12},{10,14},{6,10},{2,6},{0,2},{5,1},{9,5},... | collective-permute-start | bytes 786440 | tf_op jit(solution)/shard_map/ppermute | solution.py:429
  3.0 8.9 %collective-permute-start = (bf16[4,16,2048]{2,1,0:T(8,128)(2,1)}, bf16[4,16,2048]{2,1,0:T(8,128)(2,1)S(1)}, u32[]{:S(2)}, u32[]{:S(2)}) collective-permute-start(bf16[4,16,2048]{2,1,0:T(8,128)(2,1)} %refs_0_.1), channel_id=1, source_target_pairs={{0,4},{4,8},{8,12},{12,14},{14,10},{10,6},{6,2},{2,0},{1,5},{5,9},... | collective-permute-start | bytes 786440 | tf_op jit(solution)/shard_map/ppermute | solution.py:426
  3.8 1.2 %collective-permute-start.2 = (s32[4,128]{1,0:T(4,128)S(1)}, s32[4,128]{1,0:T(4,128)S(1)}, u32[]{:S(2)}, u32[]{:S(2)}) collective-permute-start(s32[4,128]{1,0:T(4,128)S(1)} %pad_add_fusion.notes), channel_id=1, source_target_pairs={{0,1},{1,0},{2,3},{3,2},{4,5},{5,4},{6,7},{7,6},{8,9},{9,8},{10,11... | collective-permute-start | bytes 6152 | tf_op jit(solution)/shard_map/ppermute | solution.py:386
  5.0 7.2 %copy-start.2 = (f32[2,1024]{1,0:T(2,128)S(1)}, f32[2,1024]{1,0:T(2,128)}, u32[]{:S(2)}) copy-start(f32[2,1024]{1,0:T(2,128)} %filters.1) | copy-start | bytes 24580
  8.1 5.3 %copy-start = (bf16[4,16,2048]{2,1,0:T(8,128)(2,1)S(1)}, bf16[4,16,2048]{2,1,0:T(8,128)(2,1)}, u32[]{:S(2)}) copy-start(bf16[4,16,2048]{2,1,0:T(8,128)(2,1)} %refs_0_.1) | copy-start | bytes 786436
  10.2 8.1 %collective-permute-start.6 = (bf16[4,16,2048]{2,1,0:T(8,128)(2,1)S(1)}, bf16[4,16,2048]{2,1,0:T(8,128)(2,1)S(1)}, u32[]{:S(2)}, u32[]{:S(2)}) collective-permute-start(bf16[4,16,2048]{2,1,0:T(8,128)(2,1)S(1)} %collective-permute-done.4.refs_2_), channel_id=1, source_target_pairs={{4,0},{8,4},{12,8},{14,12},{10,14},{6,10},{2,6},{0,2},{5,1},{9,5},... | collective-permute-start | bytes 786440 | tf_op jit(solution)/shard_map/ppermute | solution.py:429
  11.9 8.0 %collective-permute-start.3 = (bf16[4,16,2048]{2,1,0:T(8,128)(2,1)S(1)}, bf16[4,16,2048]{2,1,0:T(8,128)(2,1)S(1)}, u32[]{:S(2)}, u32[]{:S(2)}) collective-permute-start(bf16[4,16,2048]{2,1,0:T(8,128)(2,1)S(1)} %collective-permute-done.refs_1_), channel_id=1, source_target_pairs={{0,4},{4,8},{8,12},{12,14},{14,10},{10,6},{6,2},{2,0},{1,5},{5,9},... | collective-permute-start | bytes 786440 | tf_op jit(solution)/shard_map/ppermute | solution.py:426
  18.3 6.0 %collective-permute-start.8 = (bf16[2,16,2048]{2,1,0:T(8,128)(2,1)S(1)}, bf16[2,16,2048]{2,1,0:T(8,128)(2,1)S(1)}, u32[]{:S(2)}, u32[]{:S(2)}) collective-permute-start(bf16[2,16,2048]{2,1,0:T(8,128)(2,1)S(1)} %get-tuple-element.57), channel_id=1, source_target_pairs={{4,0},{8,4},{12,8},{14,12},{10,14},{6,10},{2,6},{0,2},{5,1},{9,5},... | collective-permute-start | bytes 393224 | tf_op jit(solution)/shard_map/ppermute | solution.py:429
  19.9 5.4 %collective-permute-start.5 = (bf16[2,16,2048]{2,1,0:T(8,128)(2,1)S(1)}, bf16[2,16,2048]{2,1,0:T(8,128)(2,1)S(1)}, u32[]{:S(2)}, u32[]{:S(2)}) collective-permute-start(bf16[2,16,2048]{2,1,0:T(8,128)(2,1)S(1)} %get-tuple-element.48), channel_id=1, source_target_pairs={{0,4},{4,8},{8,12},{12,14},{14,10},{10,6},{6,2},{2,0},{1,5},{5,9},... | collective-permute-start | bytes 393224 | tf_op jit(solution)/shard_map/ppermute | solution.py:426
  20.5 6.8 %collective-permute-start.11 = (bf16[2,16,2048]{2,1,0:T(8,128)(2,1)S(1)}, bf16[2,16,2048]{2,1,0:T(8,128)(2,1)S(1)}, u32[]{:S(2)}, u32[]{:S(2)}) collective-permute-start(bf16[2,16,2048]{2,1,0:T(8,128)(2,1)S(1)} %get-tuple-element.60), channel_id=1, source_target_pairs={{4,0},{8,4},{12,8},{14,12},{10,14},{6,10},{2,6},{0,2},{5,1},{9,5},... | collective-permute-start | bytes 393224 | tf_op jit(solution)/shard_map/ppermute | solution.py:429
  21.9 5.5 %collective-permute-start.10 = (bf16[2,16,2048]{2,1,0:T(8,128)(2,1)S(1)}, bf16[2,16,2048]{2,1,0:T(8,128)(2,1)S(1)}, u32[]{:S(2)}, u32[]{:S(2)}) collective-permute-start(bf16[2,16,2048]{2,1,0:T(8,128)(2,1)S(1)} %get-tuple-element.59), channel_id=1, source_target_pairs={{0,4},{4,8},{8,12},{12,14},{14,10},{10,6},{6,2},{2,0},{1,5},{5,9},... | collective-permute-start | bytes 393224 | tf_op jit(solution)/shard_map/ppermute | solution.py:426
  25.3 5.0 %collective-permute-start.9 = (bf16[2,16,2048]{2,1,0:T(8,128)(2,1)S(1)}, bf16[2,16,2048]{2,1,0:T(8,128)(2,1)S(1)}, u32[]{:S(2)}, u32[]{:S(2)}) collective-permute-start(bf16[2,16,2048]{2,1,0:T(8,128)(2,1)S(1)} %collective-permute-done.8.refs_3_), channel_id=1, source_target_pairs={{4,0},{8,4},{12,8},{14,12},{10,14},{6,10},{2,6},{0,2},{5,1},{9,5},... | collective-permute-start | bytes 393224 | tf_op jit(solution)/shard_map/ppermute | solution.py:429
  26.9 5.0 %collective-permute-start.7 = (bf16[2,16,2048]{2,1,0:T(8,128)(2,1)S(1)}, bf16[2,16,2048]{2,1,0:T(8,128)(2,1)S(1)}, u32[]{:S(2)}, u32[]{:S(2)}) collective-permute-start(bf16[2,16,2048]{2,1,0:T(8,128)(2,1)S(1)} %collective-permute-done.5.refs_0_), channel_id=1, source_target_pairs={{0,4},{4,8},{8,12},{12,14},{14,10},{10,6},{6,2},{2,0},{1,5},{5,9},... | collective-permute-start | bytes 393224 | tf_op jit(solution)/shard_map/ppermute | solution.py:426
  33.0 1.3 %collective-permute-start.12 = (f32[8,2048]{1,0:T(8,128)S(1)}, f32[8,2048]{1,0:T(8,128)S(1)}, u32[]{:S(2)}, u32[]{:S(2)}) collective-permute-start(f32[8,2048]{1,0:T(8,128)S(1)} %get-tuple-element.68), channel_id=1, source_target_pairs={{0,1},{1,0},{2,3},{3,2},{4,5},{5,4},{6,7},{7,6},{8,9},{9,8},{10,11... | collective-permute-start | bytes 196616 | tf_op jit(solution)/shard_map/ppermute | solution.py:386

commit v2 on v1

--- a/solution.py
+++ b/solution.py
@@ -172,7 +172,11 @@
     return [(0, part, part), (count, part, part), *full]
 
 
-def setup_kernel(per_device, aper, place, own, other, notes, notes_other, even, odd, out, token, data, arriving):
+def ring_place(chip):
+    return jnp.where(chip % 2 == 0, chip // 2, 7 - chip // 2)
+
+
+def setup_kernel(per_device, aper, ringed, rx, place, own, other, notes, notes_other, even, odd, out, token, data, arriving):
     rec_dev, samples = own.shape
     copies = [
         pltpu.make_async_copy(source, data.at[k * rec_dev : (k + 1) * rec_dev], arriving.at[k])
@@ -211,8 +215,17 @@
         slot = jnp.where(sides[side] == core, before, rec_dev + index - before)
         picks.append((slot_row == slot).astype(F32).astype(BF16))
     picks = jnp.concatenate(picks, axis=1)
-    trace = lax.broadcasted_iota(I32, (aper, aper), 0)
-    trace = trace // per_device * (2 * per_device) + core * per_device + trace % per_device
+    index = lax.broadcasted_iota(I32, (aper, aper), 0)
+    if ringed:
+        chunk, inner = index // ROWS, index % ROWS
+        offset = (chunk + 1) // 2
+        half = jnp.where((chunk % 2 == 0) & (chunk > 0), 1 - core, core)
+        spot = ring_place(rx[0]) + jnp.where(core == 0, 8 - offset, offset)
+        spot = spot % 8
+        chip = jnp.where(spot < 4, 2 * spot, 15 - 2 * spot)
+        trace = (2 * chip + half) * ROWS + inner
+    else:
+        trace = (index // per_device * 2 + core) * per_device + index % per_device
     rows = []
     for r in range(outs):
         line = lines + r % out_dev
@@ -234,12 +247,6 @@
     token[...] = jnp.zeros(token.shape, F32)
 
 
-def ring_chunk(me, offset):
-    place = jnp.where(me % 2 == 0, me // 2, 7 - me // 2)
-    place = (place + offset) % 8
-    return jnp.where(place < 4, 2 * place, 15 - 2 * place)
-
-
 def sum_rows(values):
     row = lax.broadcasted_iota(I32, values[0].shape, 0)
     for shift in (4, 2, 1):
@@ -256,24 +263,15 @@
     return values[0]
 
 
-def halves_kernel(*refs):
-    values, outs = refs[: len(refs) // 3], refs[len(refs) // 3 :]
-    cut = outs[0].shape[0]
-    for k, value in enumerate(values):
-        outs[2 * k][...] = value[:cut]
-        outs[2 * k + 1][...] = value[cut:]
-
-
-def products_kernel(offsets, count, ringed, with_total, extra, place, *refs):
+def products_kernel(chunks, count, with_total, extra, *refs):
     pieces = refs[:count]
     even, odd, spectra = refs[count : count + 3]
     totals = refs[count + 3 : count + 3 + 2 * with_total]
     outs = refs[count + 3 + 2 * with_total + extra : -1]
     work = refs[-1]
-    chunks = [ring_chunk(place[0], offset) if ringed else offset for offset in offsets]
     samples = work.shape[1]
     number = spectra.shape[1]
-    rows = work.shape[0] // len(offsets)
+    rows = work.shape[0] // len(chunks)
     sources = rows // ROWS
     data = jnp.concatenate([x[...].reshape(-1, samples) for x in pieces], axis=0)
     first = 0
@@ -287,7 +285,7 @@
             re = pl.ds(start + block * 128, 128)
             im = pl.ds(start + distance + block * 128, 128)
             sums = {}
-            for c in range(len(offsets)):
+            for c in range(len(chunks)):
                 for r in range(number):
                     right = [spectra[chunks[c], r, :, k].astype(F32) for k in (re, im)]
                     for h in range(ROWS // 8):
@@ -390,76 +388,67 @@
     fine = [pltpu.VMEM((2, FORWARD_STEP, 4 * count), F32)]
     tables = call(forward_kernel, table_shapes, "ss", fine)(rx, xl)
 
+    ringed = ring_size == 8 and own_traces == ROWS and aper == 8 * ROWS
+
     def setup():
         return call(
-            functools.partial(setup_kernel, own_traces, aper),
+            functools.partial(setup_kernel, own_traces, aper, ringed),
             [struct((chunks, outs, ROWS, samples), BF16), token],
-            "saavvvv",
+            "ssaavvvv",
             [pltpu.VMEM((2 * rec_dev, samples), BF16), pltpu.SemaphoreType.DMA((2,))],
             cost=4,
-        )(xl, records, swap(records), notes, swap(notes), *tables)
+        )(rx, xl, records, swap(records), notes, swap(notes), *tables)
 
     def arrange(filters):
         return call(filters_kernel, [struct(filters.shape, F32)], "v")(filters)[0]
 
-    def add(pieces, offsets, totals, ringed, extra=()):
+    def add(pieces, numbers, totals, extra=(), mark=True):
         kernel = functools.partial(
-            products_kernel, offsets, len(pieces), ringed, bool(totals), len(extra)
+            products_kernel, numbers, len(pieces), bool(totals), len(extra)
         )
         arguments = [*pieces, *tables, spectra, *totals, *extra]
         row_shape = struct((out_dev * sources, samples), F32)
-        kinds = "s" + "v" * len(arguments)
-        *result, done = call(
+        result = call(
             kernel,
-            [row_shape, row_shape, token],
-            kinds,
-            [pltpu.VMEM((len(offsets) * sources * ROWS, samples), F32)],
-        )(rx, *arguments)
-        return result, done
-
-    if ring_size == 8 and own_traces == ROWS:
+            [row_shape, row_shape, *[token] * mark],
+            "v" * len(arguments),
+            [pltpu.VMEM((len(numbers) * sources * ROWS, samples), F32)],
+        )(*arguments)
+        return result[:2], result[-1]
+
+    if ringed:
         order = [0, 2, 4, 6, 7, 5, 3, 1]
-        up = [(order[i], order[(i + 1) % 8]) for i in range(8)]
-        down = [(b, a) for a, b in up]
-
-        def rise(x):
-            return lax.ppermute(x, "rx", up)
-
-        def fall(x):
-            return lax.ppermute(x, "rx", down)
-
-        half = struct((sources // 2, own_traces, samples), BF16)
-
-        def halves(x):
-            return call(halves_kernel, [half] * 2, "v")(x)
-
-        a1, b1 = rise(source_traces), fall(source_traces)
+        same, cross = [], []
+        for i in range(8):
+            here, above, below = order[i], order[(i + 1) % 8], order[i - 1]
+            same += [(2 * here, 2 * above), (2 * here + 1, 2 * below + 1)]
+            cross += [(2 * here + 1, 2 * above), (2 * here, 2 * below + 1)]
+
+        def send(x, pairs=same):
+            return lax.ppermute(x, ("rx", "xl"), pairs)
+
+        a1, b1 = send(source_traces), send(source_traces, cross)
         spectra, done = setup()
-        a2, first = after(done, a1)
-        b2, second = after(done, b1)
-        a2, b2 = rise(a2), fall(b2)
-        totals, done = add([source_traces, a1, b1], [0, -1, 1], [], True, [first, second])
+        a_held, first = after(done, a1)
+        b_held, second = after(done, b1)
+        a2, b2 = send(a_held), send(b_held)
+        totals, _ = add([source_traces], [0], [], [first, second], mark=False)
+        totals, done = add([a1, b1], [1, 2], totals)
         filters = arrange(surface_filter)
-        a3, filters, first = after(done, a2, filters)
-        b3, second = after(done, b2)
-        a3_sent, a3_kept = halves(a3)
-        b3_kept, b3_sent = halves(b3)
-        a3_sent, b3_sent = rise(a3_sent), fall(b3_sent)
-        a3_kept, b3_kept = rise(a3_kept), fall(b3_kept)
-        totals, done = add([a2, b2], [-2, 2], totals, True, [first, second])
-        a4, first = after(done, a3_sent)
-        b4, second = after(done, b3_sent)
-        a4, b4 = rise(a4), fall(b4)
-        pieces = [a3_sent, a3_kept, b3_kept, b3_sent]
-        totals, _ = add(pieces, [-3, 3], totals, True, [first, second])
-        (mine, theirs), _ = add([a4, b4], [4], totals, True)
+        a_held, first = after(done, a2)
+        b_held, filters, second = after(done, b2, filters)
+        a3, b3 = send(a_held), send(b_held)
+        totals, _ = add([a2, b2], [3, 4], totals, [first, second], mark=False)
+        a4 = send(a3)
+        totals, _ = add([a3, b3], [5, 6], totals, mark=False)
+        (mine, theirs), _ = add([a4], [7], totals, mark=False)
     else:
         spectra, _ = setup()
         gathered = lax.all_gather(source_traces, "rx", axis=1, tiled=True)
         parts = [gathered[:, k * ROWS : (k + 1) * ROWS] for k in range(chunks)]
         totals = []
         for k in range(0, chunks, 2):
-            totals, _ = add(parts[k : k + 2], [k, k + 1], totals, False)
+            totals, _ = add(parts[k : k + 2], [k, k + 1], totals, mark=False)
         mine, theirs = totals
         filters = arrange(surface_filter)
 

time: 35.3 us -> 31.9 us (0.904)
  waiting for transfers between devices: 11.2 us -> 6.84 us
  starting transfers between devices: 11.5 us -> 13.5 us
  Pallas kernels: 11.7 us -> 10.5 us
    ppermute x10 -> x7, waiting for transfers between devices: 9.96 us -> 5.76 us  [send(): return lax.ppermute(x, ('rx', 'xl'), pairs)]
    ppermute x10 -> x7, starting transfers between devices: 10.9 us -> 12.6 us  [send(): return lax.ppermute(x, ('rx', 'xl'), pairs)]
    pallas_call x7 -> x6, Pallas kernels: 8.64 us -> 7.53 us  [the longest x5 4.41 us: add(): call(kernel, [row_shape, row_shape, *[token] * mark], 'v' * len(arguments...]
  transfers between devices with their start and end apart: 13 -> 10, of which waited for: 9 -> 6; matrix products, arithmetic and copies ran while one was open for 2% -> 2% of each run, Pallas kernels for 27% -> 28%
where the time goes in v2:
time: 31.9 us; the launch traced here: 31.7 us
  starting transfers between devices  13.5 us (42%)
  Pallas kernels  10.5 us (33%)
  waiting for transfers between devices  6.84 us (21%)
  other arithmetic  0.7 us (2%)
    ppermute x7, starting transfers between devices, send(): return lax.ppermute(x, ('rx', 'xl'), pairs)  12.6 us
    ppermute x7, waiting for transfers between devices, send(): return lax.ppermute(x, ('rx', 'xl'), pairs)  5.76 us
    pallas_call x5, Pallas kernels, add(): call(kernel, [row_shape, row_shape, *[token] * mark], 'v' * len(arguments...  4.41 us
    pallas_call x1, Pallas kernels, setup(): call(functools.partial(setup_kernel, own_traces, aper, ringed), [struct((...  3.12 us
    pallas_call x1, Pallas kernels, arrange(): return call(filters_kernel, [struct(filters.shape, F32)], 'v')(filters)[0]  1.12 us
    ppermute x3, waiting for transfers between devices, swap(): return lax.ppermute(x, 'xl', [(0, 1), (1, 0)])  1.08 us
    ppermute x3, starting transfers between devices, swap(): return lax.ppermute(x, 'xl', [(0, 1), (1, 0)])  0.94 us
    pallas_call x1, Pallas kernels, per_device(): call(functools.partial(finish_kernel, 1.0 / math.sqrt(aper)), [struct((so...  0.92 us
  transfers between devices with their start and end apart: 10, of which 6 were waited for; matrix products, arithmetic and copies ran while one was open for 2% of the time, Pallas kernels for 28%

profile of v2, /device:TPU:0, one launch (start us, length us, event | category | flops | bytes accessed | tf_op | source)
XLA Modules:
  0.0 31.7 jit_solution(3608360956532206551)
XLA Ops:
  0.0 0.0 copy-start
  0.0 0.5 %collective-permute-start.1 = (bf16[256,2048]{1,0:T(8,128)(2,1)}, bf16[256,2048]{1,0:T(8,128)(2,1)S(1)}, u32[]{:S(2)}, u32[]{:S(2)}) collective-permute-start(bf16[256,2048]{1,0:T(8,128)(2,1)} %own.1), channel_id=1, source_target_pairs={{0,1},{1,0},{2,3},{3,2},{4,5},{5,4},{6,7},{7,6},{8,9},{9,8},{10,11... | collective-permute-start | bytes 3145736 | tf_op jit(solution)/shard_map/ppermute | solution.py:384
  0.5 2.6 %collective-permute-start.4 = (bf16[4,16,2048]{2,1,0:T(8,128)(2,1)}, bf16[4,16,2048]{2,1,0:T(8,128)(2,1)S(1)}, u32[]{:S(2)}, u32[]{:S(2)}) collective-permute-start(bf16[4,16,2048]{2,1,0:T(8,128)(2,1)} %refs_0_.1), channel_id=1, source_target_pairs={{0,4},{1,3},{4,8},{5,1},{8,12},{9,5},{12,14},{13,9},{14,10},{15,13... | collective-permute-start | bytes 786440 | tf_op jit(solution)/shard_map/ppermute | solution.py:428
  3.1 1.3 %collective-permute-start = (bf16[4,16,2048]{2,1,0:T(8,128)(2,1)}, bf16[4,16,2048]{2,1,0:T(8,128)(2,1)S(1)}, u32[]{:S(2)}, u32[]{:S(2)}) collective-permute-start(bf16[4,16,2048]{2,1,0:T(8,128)(2,1)} %refs_0_.1), channel_id=1, source_target_pairs={{1,4},{0,3},{5,8},{4,1},{9,12},{8,5},{13,14},{12,9},{15,10},{14,13... | collective-permute-start | bytes 786440 | tf_op jit(solution)/shard_map/ppermute | solution.py:428
  4.4 0.7 %pad_add_fusion.notes = s32[4,128]{1,0:T(4,128)S(1)} fusion(s32[2,128]{1,0:T(2,128)} %param.9, s32[2,128]{1,0:T(2,128)} %bitcast.3), kind=kLoop, calls=%fused_computation | loop fusion | flops 512 | bytes 4096 | tf_op jit(solution)/shard_map/concatenate | solution.py:386
  5.1 0.4 %collective-permute-start.2 = (s32[4,128]{1,0:T(4,128)S(1)}, s32[4,128]{1,0:T(4,128)S(1)}, u32[]{:S(2)}, u32[]{:S(2)}) collective-permute-start(s32[4,128]{1,0:T(4,128)S(1)} %pad_add_fusion.notes), channel_id=1, source_target_pairs={{0,1},{1,0},{2,3},{3,2},{4,5},{5,4},{6,7},{7,6},{8,9},{9,8},{10,11... | collective-permute-start | bytes 6152 | tf_op jit(solution)/shard_map/ppermute | solution.py:384
  5.5 0.6 %shard_map.55 = (bf16[2,256,256]{2,1,0:T(8,128)(2,1)S(1)}, bf16[3,256,512]{2,1,0:T(8,128)(2,1)S(1)}) custom-call(s32[1]{0:T(128)} %bitcast.rx, s32[1]{0:T(128)} %bitcast.1.xl.place), custom_call_target="tpu_custom_call" | custom-call | flops 1000000000 | bytes 3000000 | tf_op jit(solution)/shard_map/pallas_call | solution.py:389
  6.1 0.2 collective-permute-done.2.notes_other
  6.3 0.0 collective-permute-done.1.other
  6.3 0.0 copy-done
  6.3 0.0 copy-start.1
  6.3 3.1 %shard_map.56 = (bf16[8,4,16,2048]{3,2,1,0:T(8,128)(2,1)S(1)}, f32[8,128]{1,0:T(8,128)S(1)}) custom-call(s32[1]{0:T(128)} %bitcast.rx, s32[1]{0:T(128)} %bitcast.1.xl.place, bf16[256,2048]{1,0:T(8,128)(2,1)S(1)} %copy-done, bf16[256,2048]{1,0:T(8,128)(2,1)S(1)} %collective-permute-done.1.other, s32[4,128]{1,0:T(4,128)S(1)} %pad_add_fusion.notes, ...), custom_call_target="tpu_custom_call" | custom-call | flops 4000000000 | bytes 12000000 | tf_op jit(solution)/shard_map/pallas_call | solution.py:394
  9.4 0.0 collective-permute-done.4.refs_0_
  9.4 2.0 %collective-permute-start.5 = (bf16[4,16,2048]{2,1,0:T(8,128)(2,1)S(1)}, bf16[4,16,2048]{2,1,0:T(8,128)(2,1)S(1)}, u32[]{:S(2)}, u32[]{:S(2)}) collective-permute-start(bf16[4,16,2048]{2,1,0:T(8,128)(2,1)S(1)} %collective-permute-done.4.refs_0_), channel_id=1, source_target_pairs={{0,4},{1,3},{4,8},{5,1},{8,12},{9,5},{12,14},{13,9},{14,10},{15,13... | collective-permute-start | bytes 786440 | tf_op jit(solution)/shard_map/ppermute | solution.py:428
  11.5 0.0 collective-permute-done.refs_1_
  11.5 1.6 %collective-permute-start.3 = (bf16[4,16,2048]{2,1,0:T(8,128)(2,1)S(1)}, bf16[4,16,2048]{2,1,0:T(8,128)(2,1)S(1)}, u32[]{:S(2)}, u32[]{:S(2)}) collective-permute-start(bf16[4,16,2048]{2,1,0:T(8,128)(2,1)S(1)} %collective-permute-done.refs_1_), channel_id=1, source_target_pairs={{0,4},{1,3},{4,8},{5,1},{8,12},{9,5},{12,14},{13,9},{14,10},{15,13... | collective-permute-start | bytes 786440 | tf_op jit(solution)/shard_map/ppermute | solution.py:428
  13.0 0.0 copy-done.1
  13.0 0.6 %shard_map.58 = (f32[8,2048]{1,0:T(8,128)S(1)}, f32[8,2048]{1,0:T(8,128)S(1)}) custom-call(bf16[4,16,2048]{2,1,0:T(8,128)(2,1)S(1)} %copy-done.1, bf16[2,256,256]{2,1,0:T(8,128)(2,1)S(1)} %get-tuple-element.31.even.refs_1_.refs_2_, bf16[3,256,512]{2,1,0:T(8,128)(2,1)S(1)} %get-tuple-element.32.odd.refs_2_.refs_3_, ...), custom_call_target="tpu_custom_call" | custom-call | flops 1000000000 | bytes 3000000 | tf_op jit(solution)/shard_map/pallas_call | solution.py:411
  13.7 0.0 copy-start.2
  13.7 1.1 %shard_map.59 = (f32[8,2048]{1,0:T(8,128)S(1)}, f32[8,2048]{1,0:T(8,128)S(1)}, f32[8,128]{1,0:T(8,128)S(1)}) custom-call(bf16[4,16,2048]{2,1,0:T(8,128)(2,1)S(1)} %collective-permute-done.4.refs_0_, bf16[4,16,2048]{2,1,0:T(8,128)(2,1)S(1)} %collective-permute-done.refs_1_, bf16[2,256,256]{2,1,0:T(8,128)(2,1)S(1)} %get-tuple-element.31.even.refs_1_.refs_2_, ...), custom_call_target="tpu_custom_call" | custom-call | flops 1000000000 | bytes 3000000 | tf_op jit(solution)/shard_map/pallas_call | solution.py:411
  14.7 1.4 %collective-permute-done.5.refs_0_ = bf16[4,16,2048]{2,1,0:T(8,128)(2,1)S(1)} collective-permute-done((bf16[4,16,2048]{2,1,0:T(8,128)(2,1)S(1)}, bf16[4,16,2048]{2,1,0:T(8,128)(2,1)S(1)}, u32[]{:S(2)}, u32[]{:S(2)}) %collective-permute-start.5) | collective-permute-done | bytes 262176 | tf_op jit(solution)/shard_map/ppermute | solution.py:428
  16.1 1.7 %collective-permute-start.6 = (bf16[4,16,2048]{2,1,0:T(8,128)(2,1)S(1)}, bf16[4,16,2048]{2,1,0:T(8,128)(2,1)S(1)}, u32[]{:S(2)}, u32[]{:S(2)}) collective-permute-start(bf16[4,16,2048]{2,1,0:T(8,128)(2,1)S(1)} %collective-permute-done.5.refs_0_), channel_id=1, source_target_pairs={{0,4},{1,3},{4,8},{5,1},{8,12},{9,5},{12,14},{13,9},{14,10},{15,13... | collective-permute-start | bytes 786440 | tf_op jit(solution)/shard_map/ppermute | solution.py:428
  17.8 0.0 copy-done.2
  17.8 1.1 %shard_map.57.filters = f32[2,1024]{1,0:T(2,128)S(1)} custom-call(f32[2,1024]{1,0:T(2,128)S(1)} %copy-done.2), custom_call_target="tpu_custom_call" | custom-call | flops 1000000000 | bytes 3000000 | tf_op jit(solution)/shard_map/pallas_call | solution.py:403
  19.0 0.0 collective-permute-done.3.refs_1_
  19.0 1.7 %collective-permute-start.8 = (bf16[4,16,2048]{2,1,0:T(8,128)(2,1)S(1)}, bf16[4,16,2048]{2,1,0:T(8,128)(2,1)S(1)}, u32[]{:S(2)}, u32[]{:S(2)}) collective-permute-start(bf16[4,16,2048]{2,1,0:T(8,128)(2,1)S(1)} %collective-permute-done.3.refs_1_), channel_id=1, source_target_pairs={{0,4},{1,3},{4,8},{5,1},{8,12},{9,5},{12,14},{13,9},{14,10},{15,13... | collective-permute-start | bytes 786440 | tf_op jit(solution)/shard_map/ppermute | solution.py:428
  20.6 1.9 %collective-permute-done.6.refs_0_ = bf16[4,16,2048]{2,1,0:T(8,128)(2,1)S(1)} collective-permute-done((bf16[4,16,2048]{2,1,0:T(8,128)(2,1)S(1)}, bf16[4,16,2048]{2,1,0:T(8,128)(2,1)S(1)}, u32[]{:S(2)}, u32[]{:S(2)}) %collective-permute-start.6) | collective-permute-done | bytes 262176 | tf_op jit(solution)/shard_map/ppermute | solution.py:428
  22.5 1.7 %collective-permute-start.7 = (bf16[4,16,2048]{2,1,0:T(8,128)(2,1)S(1)}, bf16[4,16,2048]{2,1,0:T(8,128)(2,1)S(1)}, u32[]{:S(2)}, u32[]{:S(2)}) collective-permute-start(bf16[4,16,2048]{2,1,0:T(8,128)(2,1)S(1)} %collective-permute-done.6.refs_0_), channel_id=1, source_target_pairs={{0,4},{1,3},{4,8},{5,1},{8,12},{9,5},{12,14},{13,9},{14,10},{15,13... | collective-permute-start | bytes 786440 | tf_op jit(solution)/shard_map/ppermute | solution.py:428
  24.2 1.1 %shard_map.60 = (f32[8,2048]{1,0:T(8,128)S(1)}, f32[8,2048]{1,0:T(8,128)S(1)}) custom-call(bf16[4,16,2048]{2,1,0:T(8,128)(2,1)S(1)} %collective-permute-done.5.refs_0_, bf16[4,16,2048]{2,1,0:T(8,128)(2,1)S(1)} %collective-permute-done.3.refs_1_, bf16[2,256,256]{2,1,0:T(8,128)(2,1)S(1)} %get-tuple-element.31.even.refs_1_.refs_2_, ...), custom_call_target="tpu_custom_call" | custom-call | flops 1000000000 | bytes 3000000 | tf_op jit(solution)/shard_map/pallas_call | solution.py:411
  25.3 0.1 collective-permute-done.8.refs_1_
  25.4 1.1 %shard_map.61 = (f32[8,2048]{1,0:T(8,128)S(1)}, f32[8,2048]{1,0:T(8,128)S(1)}) custom-call(bf16[4,16,2048]{2,1,0:T(8,128)(2,1)S(1)} %collective-permute-done.6.refs_0_, bf16[4,16,2048]{2,1,0:T(8,128)(2,1)S(1)} %collective-permute-done.8.refs_1_, bf16[2,256,256]{2,1,0:T(8,128)(2,1)S(1)} %get-tuple-element.31.even.refs_1_.refs_2_, ...), custom_call_target="tpu_custom_call" | custom-call | flops 1000000000 | bytes 3000000 | tf_op jit(solution)/shard_map/pallas_call | solution.py:411
  26.5 2.4 %collective-permute-done.7.refs_0_ = bf16[4,16,2048]{2,1,0:T(8,128)(2,1)S(1)} collective-permute-done((bf16[4,16,2048]{2,1,0:T(8,128)(2,1)S(1)}, bf16[4,16,2048]{2,1,0:T(8,128)(2,1)S(1)}, u32[]{:S(2)}, u32[]{:S(2)}) %collective-permute-start.7) | collective-permute-done | bytes 262176 | tf_op jit(solution)/shard_map/ppermute | solution.py:428
  28.9 0.6 %shard_map.62 = (f32[8,2048]{1,0:T(8,128)S(1)}, f32[8,2048]{1,0:T(8,128)S(1)}) custom-call(bf16[4,16,2048]{2,1,0:T(8,128)(2,1)S(1)} %collective-permute-done.7.refs_0_, bf16[2,256,256]{2,1,0:T(8,128)(2,1)S(1)} %get-tuple-element.31.even.refs_1_.refs_2_, bf16[3,256,512]{2,1,0:T(8,128)(2,1)S(1)} %get-tuple-element.32.odd.refs_2_.refs_3_, ...), custom_call_target="tpu_custom_call" | custom-call | flops 1000000000 | bytes 3000000 | tf_op jit(solution)/shard_map/pallas_call | solution.py:411
  29.5 0.1 collective-permute-start.9
  29.6 0.3 %shard_map.63 = (bf16[2,256,256]{2,1,0:T(8,128)(2,1)S(1)}, bf16[3,256,512]{2,1,0:T(8,128)(2,1)S(1)}) custom-call(), custom_call_target="tpu_custom_call" | custom-call | flops 1000000000 | bytes 3000000 | tf_op jit(solution)/shard_map/pallas_call | solution.py:456
  29.9 0.9 %collective-permute-done.9.arrived = f32[8,2048]{1,0:T(8,128)S(1)} collective-permute-done((f32[8,2048]{1,0:T(8,128)S(1)}, f32[8,2048]{1,0:T(8,128)S(1)}, u32[]{:S(2)}, u32[]{:S(2)}) %collective-permute-start.9) | collective-permute-done | bytes 65568 | tf_op jit(solution)/shard_map/ppermute | solution.py:384
  30.8 0.9 %shard_map.64 = bf16[4,2,2048]{2,1,0:T(2,128)(2,1)} custom-call(f32[2,1024]{1,0:T(2,128)S(1)} %shard_map.57.filters, f32[8,2048]{1,0:T(8,128)S(1)} %get-tuple-element.53.mine, f32[8,2048]{1,0:T(8,128)S(1)} %collective-permute-done.9.arrived, bf16[2,256,256]{2,1,0:T(8,128)(2,1)S(1)} %get-tuple-element.55.even, bf16[3,256,512]{2,1,0:T(8,128)(2,1)S(1)} %get-tuple-element.56.odd), custom_call_target="tpu_custom_call" | custom-call | flops 1000000000 | bytes 3000000 | tf_op jit(solution)/shard_map/pallas_call | solution.py:457
Async XLA Ops:
  0.0 6.3 %copy-start = (bf16[256,2048]{1,0:T(8,128)(2,1)S(1)}, bf16[256,2048]{1,0:T(8,128)(2,1)}, u32[]{:S(2)}) copy-start(bf16[256,2048]{1,0:T(8,128)(2,1)} %own.1) | copy-start | bytes 3145732
  0.0 6.3 %collective-permute-start.1 = (bf16[256,2048]{1,0:T(8,128)(2,1)}, bf16[256,2048]{1,0:T(8,128)(2,1)S(1)}, u32[]{:S(2)}, u32[]{:S(2)}) collective-permute-start(bf16[256,2048]{1,0:T(8,128)(2,1)} %own.1), channel_id=1, source_target_pairs={{0,1},{1,0},{2,3},{3,2},{4,5},{5,4},{6,7},{7,6},{8,9},{9,8},{10,11... | collective-permute-start | bytes 3145736 | tf_op jit(solution)/shard_map/ppermute | solution.py:384
  0.5 9.0 %collective-permute-start.4 = (bf16[4,16,2048]{2,1,0:T(8,128)(2,1)}, bf16[4,16,2048]{2,1,0:T(8,128)(2,1)S(1)}, u32[]{:S(2)}, u32[]{:S(2)}) collective-permute-start(bf16[4,16,2048]{2,1,0:T(8,128)(2,1)} %refs_0_.1), channel_id=1, source_target_pairs={{0,4},{1,3},{4,8},{5,1},{8,12},{9,5},{12,14},{13,9},{14,10},{15,13... | collective-permute-start | bytes 786440 | tf_op jit(solution)/shard_map/ppermute | solution.py:428
  3.1 8.4 %collective-permute-start = (bf16[4,16,2048]{2,1,0:T(8,128)(2,1)}, bf16[4,16,2048]{2,1,0:T(8,128)(2,1)S(1)}, u32[]{:S(2)}, u32[]{:S(2)}) collective-permute-start(bf16[4,16,2048]{2,1,0:T(8,128)(2,1)} %refs_0_.1), channel_id=1, source_target_pairs={{1,4},{0,3},{5,8},{4,1},{9,12},{8,5},{13,14},{12,9},{15,10},{14,13... | collective-permute-start | bytes 786440 | tf_op jit(solution)/shard_map/ppermute | solution.py:428
  5.1 1.2 %collective-permute-start.2 = (s32[4,128]{1,0:T(4,128)S(1)}, s32[4,128]{1,0:T(4,128)S(1)}, u32[]{:S(2)}, u32[]{:S(2)}) collective-permute-start(s32[4,128]{1,0:T(4,128)S(1)} %pad_add_fusion.notes), channel_id=1, source_target_pairs={{0,1},{1,0},{2,3},{3,2},{4,5},{5,4},{6,7},{7,6},{8,9},{9,8},{10,11... | collective-permute-start | bytes 6152 | tf_op jit(solution)/shard_map/ppermute | solution.py:384
  6.3 6.7 %copy-start.1 = (bf16[4,16,2048]{2,1,0:T(8,128)(2,1)S(1)}, bf16[4,16,2048]{2,1,0:T(8,128)(2,1)}, u32[]{:S(2)}) copy-start(bf16[4,16,2048]{2,1,0:T(8,128)(2,1)} %refs_0_.1) | copy-start | bytes 786436
  9.4 6.7 %collective-permute-start.5 = (bf16[4,16,2048]{2,1,0:T(8,128)(2,1)S(1)}, bf16[4,16,2048]{2,1,0:T(8,128)(2,1)S(1)}, u32[]{:S(2)}, u32[]{:S(2)}) collective-permute-start(bf16[4,16,2048]{2,1,0:T(8,128)(2,1)S(1)} %collective-permute-done.4.refs_0_), channel_id=1, source_target_pairs={{0,4},{1,3},{4,8},{5,1},{8,12},{9,5},{12,14},{13,9},{14,10},{15,13... | collective-permute-start | bytes 786440 | tf_op jit(solution)/shard_map/ppermute | solution.py:428
  11.5 7.5 %collective-permute-start.3 = (bf16[4,16,2048]{2,1,0:T(8,128)(2,1)S(1)}, bf16[4,16,2048]{2,1,0:T(8,128)(2,1)S(1)}, u32[]{:S(2)}, u32[]{:S(2)}) collective-permute-start(bf16[4,16,2048]{2,1,0:T(8,128)(2,1)S(1)} %collective-permute-done.refs_1_), channel_id=1, source_target_pairs={{0,4},{1,3},{4,8},{5,1},{8,12},{9,5},{12,14},{13,9},{14,10},{15,13... | collective-permute-start | bytes 786440 | tf_op jit(solution)/shard_map/ppermute | solution.py:428
  13.7 4.2 %copy-start.2 = (f32[2,1024]{1,0:T(2,128)S(1)}, f32[2,1024]{1,0:T(2,128)}, u32[]{:S(2)}) copy-start(f32[2,1024]{1,0:T(2,128)} %filters.1) | copy-start | bytes 24580
  16.1 6.4 %collective-permute-start.6 = (bf16[4,16,2048]{2,1,0:T(8,128)(2,1)S(1)}, bf16[4,16,2048]{2,1,0:T(8,128)(2,1)S(1)}, u32[]{:S(2)}, u32[]{:S(2)}) collective-permute-start(bf16[4,16,2048]{2,1,0:T(8,128)(2,1)S(1)} %collective-permute-done.5.refs_0_), channel_id=1, source_target_pairs={{0,4},{1,3},{4,8},{5,1},{8,12},{9,5},{12,14},{13,9},{14,10},{15,13... | collective-permute-start | bytes 786440 | tf_op jit(solution)/shard_map/ppermute | solution.py:428
  19.0 6.4 %collective-permute-start.8 = (bf16[4,16,2048]{2,1,0:T(8,128)(2,1)S(1)}, bf16[4,16,2048]{2,1,0:T(8,128)(2,1)S(1)}, u32[]{:S(2)}, u32[]{:S(2)}) collective-permute-start(bf16[4,16,2048]{2,1,0:T(8,128)(2,1)S(1)} %collective-permute-done.3.refs_1_), channel_id=1, source_target_pairs={{0,4},{1,3},{4,8},{5,1},{8,12},{9,5},{12,14},{13,9},{14,10},{15,13... | collective-permute-start | bytes 786440 | tf_op jit(solution)/shard_map/ppermute | solution.py:428
  22.5 6.4 %collective-permute-start.7 = (bf16[4,16,2048]{2,1,0:T(8,128)(2,1)S(1)}, bf16[4,16,2048]{2,1,0:T(8,128)(2,1)S(1)}, u32[]{:S(2)}, u32[]{:S(2)}) collective-permute-start(bf16[4,16,2048]{2,1,0:T(8,128)(2,1)S(1)} %collective-permute-done.6.refs_0_), channel_id=1, source_target_pairs={{0,4},{1,3},{4,8},{5,1},{8,12},{9,5},{12,14},{13,9},{14,10},{15,13... | collective-permute-start | bytes 786440 | tf_op jit(solution)/shard_map/ppermute | solution.py:428
  29.5 1.3 %collective-permute-start.9 = (f32[8,2048]{1,0:T(8,128)S(1)}, f32[8,2048]{1,0:T(8,128)S(1)}, u32[]{:S(2)}, u32[]{:S(2)}) collective-permute-start(f32[8,2048]{1,0:T(8,128)S(1)} %get-tuple-element.54), channel_id=1, source_target_pairs={{0,1},{1,0},{2,3},{3,2},{4,5},{5,4},{6,7},{7,6},{8,9},{9,8},{10,11... | collective-permute-start | bytes 196616 | tf_op jit(solution)/shard_map/ppermute | solution.py:384

commit v3 on v2

--- a/solution.py
+++ b/solution.py
@@ -176,14 +176,8 @@
     return jnp.where(chip % 2 == 0, chip // 2, 7 - chip // 2)
 
 
-def setup_kernel(per_device, aper, ringed, rx, place, own, other, notes, notes_other, even, odd, out, token, data, arriving):
+def setup_kernel(per_device, aper, ringed, rx, place, own, other, notes, notes_other, even, odd, out, token):
     rec_dev, samples = own.shape
-    copies = [
-        pltpu.make_async_copy(source, data.at[k * rec_dev : (k + 1) * rec_dev], arriving.at[k])
-        for k, source in enumerate((own, other))
-    ]
-    for copy in copies:
-        copy.start()
     core = place[0]
     slots = 2 * rec_dev
     outs = slots // aper
@@ -234,9 +228,9 @@
         pick = picks[r * aper : (r + 1) * aper]
         rows.append(jnp.dot(match, pick, preferred_element_type=F32).astype(BF16))
     placed = jnp.concatenate(rows, axis=0)
-    for copy in copies:
-        copy.wait()
-    routed = jnp.dot(placed, data[...], preferred_element_type=F32)
+    routed = jnp.dot(placed[:, :rec_dev], own[...], preferred_element_type=F32) + jnp.dot(
+        placed[:, rec_dev:], other[...], preferred_element_type=F32
+    )
     first = 0
     for block in transform(split(routed), even, odd):
         width = block.shape[1]
@@ -394,8 +388,7 @@
         return call(
             functools.partial(setup_kernel, own_traces, aper, ringed),
             [struct((chunks, outs, ROWS, samples), BF16), token],
-            "ssaavvvv",
-            [pltpu.VMEM((2 * rec_dev, samples), BF16), pltpu.SemaphoreType.DMA((2,))],
+            "ssvvvvvv",
             cost=4,
         )(rx, xl, records, swap(records), notes, swap(notes), *tables)
 
@@ -430,10 +423,11 @@
         a1, b1 = send(source_traces), send(source_traces, cross)
         spectra, done = setup()
         a_held, first = after(done, a1)
+        a2 = send(a_held)
+        totals, done = add([source_traces], [0], [], [first])
         b_held, second = after(done, b1)
-        a2, b2 = send(a_held), send(b_held)
-        totals, _ = add([source_traces], [0], [], [first, second], mark=False)
-        totals, done = add([a1, b1], [1, 2], totals)
+        b2 = send(b_held)
+        totals, done = add([a1, b1], [1, 2], totals, [second])
         filters = arrange(surface_filter)
         a_held, first = after(done, a2)
         b_held, filters, second = after(done, b2, filters)

time: 31.9 us -> 31.9 us (level)
  starting transfers between devices: 13.5 us -> 13.9 us
    ppermute x7, starting transfers between devices: 12.6 us -> 12.9 us  [send(): return lax.ppermute(x, ('rx', 'xl'), pairs)]
  transfers between devices with their start and end apart: 10 -> 10, of which waited for: 6 -> 6; matrix products, arithmetic and copies ran while one was open for 2% -> 2% of each run, Pallas kernels for 28% -> 27%
where the time goes in v3:
time: 31.9 us; the launch traced here: 31.7 us
  starting transfers between devices  13.9 us (44%)
  Pallas kernels  10.2 us (32%)
  waiting for transfers between devices  6.87 us (22%)
  other arithmetic  0.7 us (2%)
    ppermute x7, starting transfers between devices, send(): return lax.ppermute(x, ('rx', 'xl'), pairs)  12.9 us
    ppermute x7, waiting for transfers between devices, send(): return lax.ppermute(x, ('rx', 'xl'), pairs)  5.78 us
    pallas_call x5, Pallas kernels, add(): call(kernel, [row_shape, row_shape, *[token] * mark], 'v' * len(arguments...  4.32 us
    pallas_call x1, Pallas kernels, setup(): call(functools.partial(setup_kernel, own_traces, aper, ringed), [struct((...  2.82 us
    pallas_call x1, Pallas kernels, arrange(): return call(filters_kernel, [struct(filters.shape, F32)], 'v')(filters)[0]  1.12 us
    ppermute x3, waiting for transfers between devices, swap(): return lax.ppermute(x, 'xl', [(0, 1), (1, 0)])  1.08 us
    ppermute x3, starting transfers between devices, swap(): return lax.ppermute(x, 'xl', [(0, 1), (1, 0)])  0.94 us
    pallas_call x1, Pallas kernels, per_device(): call(functools.partial(finish_kernel, 1.0 / math.sqrt(aper)), [struct((so...  0.92 us
  transfers between devices with their start and end apart: 10, of which 6 were waited for; matrix products, arithmetic and copies ran while one was open for 2% of the time, Pallas kernels for 27%

profile of v3, /device:TPU:0, one launch (start us, length us, event | category | flops | bytes accessed | tf_op | source)
XLA Modules:
  0.0 31.7 jit_solution(15117128060724621729)
XLA Ops:
  0.0 0.0 copy-start
  0.0 0.5 %collective-permute-start.1 = (bf16[256,2048]{1,0:T(8,128)(2,1)}, bf16[256,2048]{1,0:T(8,128)(2,1)S(1)}, u32[]{:S(2)}, u32[]{:S(2)}) collective-permute-start(bf16[256,2048]{1,0:T(8,128)(2,1)} %own.1), channel_id=1, source_target_pairs={{0,1},{1,0},{2,3},{3,2},{4,5},{5,4},{6,7},{7,6},{8,9},{9,8},{10,11... | collective-permute-start | bytes 3145736 | tf_op jit(solution)/shard_map/ppermute | solution.py:378
  0.5 2.6 %collective-permute-start.3 = (bf16[4,16,2048]{2,1,0:T(8,128)(2,1)}, bf16[4,16,2048]{2,1,0:T(8,128)(2,1)S(1)}, u32[]{:S(2)}, u32[]{:S(2)}) collective-permute-start(bf16[4,16,2048]{2,1,0:T(8,128)(2,1)} %refs_0_.1), channel_id=1, source_target_pairs={{0,4},{1,3},{4,8},{5,1},{8,12},{9,5},{12,14},{13,9},{14,10},{15,13... | collective-permute-start | bytes 786440 | tf_op jit(solution)/shard_map/ppermute | solution.py:421
  3.1 1.3 %collective-permute-start = (bf16[4,16,2048]{2,1,0:T(8,128)(2,1)}, bf16[4,16,2048]{2,1,0:T(8,128)(2,1)S(1)}, u32[]{:S(2)}, u32[]{:S(2)}) collective-permute-start(bf16[4,16,2048]{2,1,0:T(8,128)(2,1)} %refs_0_.1), channel_id=1, source_target_pairs={{1,4},{0,3},{5,8},{4,1},{9,12},{8,5},{13,14},{12,9},{15,10},{14,13... | collective-permute-start | bytes 786440 | tf_op jit(solution)/shard_map/ppermute | solution.py:421
  4.4 0.7 %pad_add_fusion.notes = s32[4,128]{1,0:T(4,128)S(1)} fusion(s32[2,128]{1,0:T(2,128)} %param.9, s32[2,128]{1,0:T(2,128)} %bitcast.3), kind=kLoop, calls=%fused_computation | loop fusion | flops 512 | bytes 4096 | tf_op jit(solution)/shard_map/concatenate | solution.py:380
  5.1 0.4 %collective-permute-start.2 = (s32[4,128]{1,0:T(4,128)S(1)}, s32[4,128]{1,0:T(4,128)S(1)}, u32[]{:S(2)}, u32[]{:S(2)}) collective-permute-start(s32[4,128]{1,0:T(4,128)S(1)} %pad_add_fusion.notes), channel_id=1, source_target_pairs={{0,1},{1,0},{2,3},{3,2},{4,5},{5,4},{6,7},{7,6},{8,9},{9,8},{10,11... | collective-permute-start | bytes 6152 | tf_op jit(solution)/shard_map/ppermute | solution.py:378
  5.5 0.6 %shard_map.55 = (bf16[2,256,256]{2,1,0:T(8,128)(2,1)S(1)}, bf16[3,256,512]{2,1,0:T(8,128)(2,1)S(1)}) custom-call(s32[1]{0:T(128)} %bitcast.rx, s32[1]{0:T(128)} %bitcast.1.xl.place), custom_call_target="tpu_custom_call" | custom-call | flops 1000000000 | bytes 3000000 | tf_op jit(solution)/shard_map/pallas_call | solution.py:383
  6.1 0.2 collective-permute-done.2.notes_other
  6.3 0.0 collective-permute-done.1.other
  6.3 0.0 copy-done
  6.3 0.0 copy-start.1
  6.3 2.8 %shard_map.56 = (bf16[8,4,16,2048]{3,2,1,0:T(8,128)(2,1)S(1)}, f32[8,128]{1,0:T(8,128)S(1)}) custom-call(s32[1]{0:T(128)} %bitcast.rx, s32[1]{0:T(128)} %bitcast.1.xl.place, bf16[256,2048]{1,0:T(8,128)(2,1)S(1)} %copy-done, bf16[256,2048]{1,0:T(8,128)(2,1)S(1)} %collective-permute-done.1.other, s32[4,128]{1,0:T(4,128)S(1)} %pad_add_fusion.notes, ...), custom_call_target="tpu_custom_call" | custom-call | flops 4000000000 | bytes 12000000 | tf_op jit(solution)/shard_map/pallas_call | solution.py:388
  9.1 0.0 collective-permute-done.3.refs_0_
  9.1 2.3 %collective-permute-start.5 = (bf16[4,16,2048]{2,1,0:T(8,128)(2,1)S(1)}, bf16[4,16,2048]{2,1,0:T(8,128)(2,1)S(1)}, u32[]{:S(2)}, u32[]{:S(2)}) collective-permute-start(bf16[4,16,2048]{2,1,0:T(8,128)(2,1)S(1)} %collective-permute-done.3.refs_0_), channel_id=1, source_target_pairs={{0,4},{1,3},{4,8},{5,1},{8,12},{9,5},{12,14},{13,9},{14,10},{15,13... | collective-permute-start | bytes 786440 | tf_op jit(solution)/shard_map/ppermute | solution.py:421
  11.5 0.0 copy-done.1
  11.5 0.6 %shard_map.57 = (f32[8,2048]{1,0:T(8,128)S(1)}, f32[8,2048]{1,0:T(8,128)S(1)}, f32[8,128]{1,0:T(8,128)S(1)}) custom-call(bf16[4,16,2048]{2,1,0:T(8,128)(2,1)S(1)} %copy-done.1, bf16[2,256,256]{2,1,0:T(8,128)(2,1)S(1)} %get-tuple-element.32.even.refs_1_.refs_2_, bf16[3,256,512]{2,1,0:T(8,128)(2,1)S(1)} %get-tuple-element.33.odd.refs_2_.refs_3_, ...), custom_call_target="tpu_custom_call" | custom-call | flops 1000000000 | bytes 3000000 | tf_op jit(solution)/shard_map/pallas_call | solution.py:404
  12.1 0.0 copy-start.2
  12.1 0.0 collective-permute-done.refs_1_
  12.1 1.6 %collective-permute-start.4 = (bf16[4,16,2048]{2,1,0:T(8,128)(2,1)S(1)}, bf16[4,16,2048]{2,1,0:T(8,128)(2,1)S(1)}, u32[]{:S(2)}, u32[]{:S(2)}) collective-permute-start(bf16[4,16,2048]{2,1,0:T(8,128)(2,1)S(1)} %collective-permute-done.refs_1_), channel_id=1, source_target_pairs={{0,4},{1,3},{4,8},{5,1},{8,12},{9,5},{12,14},{13,9},{14,10},{15,13... | collective-permute-start | bytes 786440 | tf_op jit(solution)/shard_map/ppermute | solution.py:421
  13.7 1.0 %shard_map.59 = (f32[8,2048]{1,0:T(8,128)S(1)}, f32[8,2048]{1,0:T(8,128)S(1)}, f32[8,128]{1,0:T(8,128)S(1)}) custom-call(bf16[4,16,2048]{2,1,0:T(8,128)(2,1)S(1)} %collective-permute-done.3.refs_0_, bf16[4,16,2048]{2,1,0:T(8,128)(2,1)S(1)} %collective-permute-done.refs_1_, bf16[2,256,256]{2,1,0:T(8,128)(2,1)S(1)} %get-tuple-element.32.even.refs_1_.refs_2_, ...), custom_call_target="tpu_custom_call" | custom-call | flops 1000000000 | bytes 3000000 | tf_op jit(solution)/shard_map/pallas_call | solution.py:404
  14.8 1.4 %collective-permute-done.5.refs_0_ = bf16[4,16,2048]{2,1,0:T(8,128)(2,1)S(1)} collective-permute-done((bf16[4,16,2048]{2,1,0:T(8,128)(2,1)S(1)}, bf16[4,16,2048]{2,1,0:T(8,128)(2,1)S(1)}, u32[]{:S(2)}, u32[]{:S(2)}) %collective-permute-start.5) | collective-permute-done | bytes 262176 | tf_op jit(solution)/shard_map/ppermute | solution.py:421
  16.1 1.7 %collective-permute-start.6 = (bf16[4,16,2048]{2,1,0:T(8,128)(2,1)S(1)}, bf16[4,16,2048]{2,1,0:T(8,128)(2,1)S(1)}, u32[]{:S(2)}, u32[]{:S(2)}) collective-permute-start(bf16[4,16,2048]{2,1,0:T(8,128)(2,1)S(1)} %collective-permute-done.5.refs_0_), channel_id=1, source_target_pairs={{0,4},{1,3},{4,8},{5,1},{8,12},{9,5},{12,14},{13,9},{14,10},{15,13... | collective-permute-start | bytes 786440 | tf_op jit(solution)/shard_map/ppermute | solution.py:421
  17.8 0.0 copy-done.2
  17.8 1.1 %shard_map.58.filters = f32[2,1024]{1,0:T(2,128)S(1)} custom-call(f32[2,1024]{1,0:T(2,128)S(1)} %copy-done.2), custom_call_target="tpu_custom_call" | custom-call | flops 1000000000 | bytes 3000000 | tf_op jit(solution)/shard_map/pallas_call | solution.py:396
  19.0 0.0 collective-permute-done.4.refs_1_
  19.0 1.7 %collective-permute-start.8 = (bf16[4,16,2048]{2,1,0:T(8,128)(2,1)S(1)}, bf16[4,16,2048]{2,1,0:T(8,128)(2,1)S(1)}, u32[]{:S(2)}, u32[]{:S(2)}) collective-permute-start(bf16[4,16,2048]{2,1,0:T(8,128)(2,1)S(1)} %collective-permute-done.4.refs_1_), channel_id=1, source_target_pairs={{0,4},{1,3},{4,8},{5,1},{8,12},{9,5},{12,14},{13,9},{14,10},{15,13... | collective-permute-start | bytes 786440 | tf_op jit(solution)/shard_map/ppermute | solution.py:421
  20.6 1.9 %collective-permute-done.6.refs_0_ = bf16[4,16,2048]{2,1,0:T(8,128)(2,1)S(1)} collective-permute-done((bf16[4,16,2048]{2,1,0:T(8,128)(2,1)S(1)}, bf16[4,16,2048]{2,1,0:T(8,128)(2,1)S(1)}, u32[]{:S(2)}, u32[]{:S(2)}) %collective-permute-start.6) | collective-permute-done | bytes 262176 | tf_op jit(solution)/shard_map/ppermute | solution.py:421
  22.5 1.7 %collective-permute-start.7 = (bf16[4,16,2048]{2,1,0:T(8,128)(2,1)S(1)}, bf16[4,16,2048]{2,1,0:T(8,128)(2,1)S(1)}, u32[]{:S(2)}, u32[]{:S(2)}) collective-permute-start(bf16[4,16,2048]{2,1,0:T(8,128)(2,1)S(1)} %collective-permute-done.6.refs_0_), channel_id=1, source_target_pairs={{0,4},{1,3},{4,8},{5,1},{8,12},{9,5},{12,14},{13,9},{14,10},{15,13... | collective-permute-start | bytes 786440 | tf_op jit(solution)/shard_map/ppermute | solution.py:421
  24.2 1.0 %shard_map.60 = (f32[8,2048]{1,0:T(8,128)S(1)}, f32[8,2048]{1,0:T(8,128)S(1)}) custom-call(bf16[4,16,2048]{2,1,0:T(8,128)(2,1)S(1)} %collective-permute-done.5.refs_0_, bf16[4,16,2048]{2,1,0:T(8,128)(2,1)S(1)} %collective-permute-done.4.refs_1_, bf16[2,256,256]{2,1,0:T(8,128)(2,1)S(1)} %get-tuple-element.32.even.refs_1_.refs_2_, ...), custom_call_target="tpu_custom_call" | custom-call | flops 1000000000 | bytes 3000000 | tf_op jit(solution)/shard_map/pallas_call | solution.py:404
  25.3 0.1 collective-permute-done.8.refs_1_
  25.4 1.0 %shard_map.61 = (f32[8,2048]{1,0:T(8,128)S(1)}, f32[8,2048]{1,0:T(8,128)S(1)}) custom-call(bf16[4,16,2048]{2,1,0:T(8,128)(2,1)S(1)} %collective-permute-done.6.refs_0_, bf16[4,16,2048]{2,1,0:T(8,128)(2,1)S(1)} %collective-permute-done.8.refs_1_, bf16[2,256,256]{2,1,0:T(8,128)(2,1)S(1)} %get-tuple-element.32.even.refs_1_.refs_2_, ...), custom_call_target="tpu_custom_call" | custom-call | flops 1000000000 | bytes 3000000 | tf_op jit(solution)/shard_map/pallas_call | solution.py:404
  26.4 2.4 %collective-permute-done.7.refs_0_ = bf16[4,16,2048]{2,1,0:T(8,128)(2,1)S(1)} collective-permute-done((bf16[4,16,2048]{2,1,0:T(8,128)(2,1)S(1)}, bf16[4,16,2048]{2,1,0:T(8,128)(2,1)S(1)}, u32[]{:S(2)}, u32[]{:S(2)}) %collective-permute-start.7) | collective-permute-done | bytes 262176 | tf_op jit(solution)/shard_map/ppermute | solution.py:421
  28.9 0.6 %shard_map.62 = (f32[8,2048]{1,0:T(8,128)S(1)}, f32[8,2048]{1,0:T(8,128)S(1)}) custom-call(bf16[4,16,2048]{2,1,0:T(8,128)(2,1)S(1)} %collective-permute-done.7.refs_0_, bf16[2,256,256]{2,1,0:T(8,128)(2,1)S(1)} %get-tuple-element.32.even.refs_1_.refs_2_, bf16[3,256,512]{2,1,0:T(8,128)(2,1)S(1)} %get-tuple-element.33.odd.refs_2_.refs_3_, ...), custom_call_target="tpu_custom_call" | custom-call | flops 1000000000 | bytes 3000000 | tf_op jit(solution)/shard_map/pallas_call | solution.py:404
  29.5 0.1 collective-permute-start.9
  29.6 0.3 %shard_map.63 = (bf16[2,256,256]{2,1,0:T(8,128)(2,1)S(1)}, bf16[3,256,512]{2,1,0:T(8,128)(2,1)S(1)}) custom-call(), custom_call_target="tpu_custom_call" | custom-call | flops 1000000000 | bytes 3000000 | tf_op jit(solution)/shard_map/pallas_call | solution.py:450
  29.9 0.9 %collective-permute-done.9.arrived = f32[8,2048]{1,0:T(8,128)S(1)} collective-permute-done((f32[8,2048]{1,0:T(8,128)S(1)}, f32[8,2048]{1,0:T(8,128)S(1)}, u32[]{:S(2)}, u32[]{:S(2)}) %collective-permute-start.9) | collective-permute-done | bytes 65568 | tf_op jit(solution)/shard_map/ppermute | solution.py:378
  30.8 0.9 %shard_map.64 = bf16[4,2,2048]{2,1,0:T(2,128)(2,1)} custom-call(f32[2,1024]{1,0:T(2,128)S(1)} %shard_map.58.filters, f32[8,2048]{1,0:T(8,128)S(1)} %get-tuple-element.55.mine, f32[8,2048]{1,0:T(8,128)S(1)} %collective-permute-done.9.arrived, bf16[2,256,256]{2,1,0:T(8,128)(2,1)S(1)} %get-tuple-element.57.even, bf16[3,256,512]{2,1,0:T(8,128)(2,1)S(1)} %get-tuple-element.58.odd), custom_call_target="tpu_custom_call" | custom-call | flops 1000000000 | bytes 3000000 | tf_op jit(solution)/shard_map/pallas_call | solution.py:451
Async XLA Ops:
  0.0 6.3 %copy-start = (bf16[256,2048]{1,0:T(8,128)(2,1)S(1)}, bf16[256,2048]{1,0:T(8,128)(2,1)}, u32[]{:S(2)}) copy-start(bf16[256,2048]{1,0:T(8,128)(2,1)} %own.1) | copy-start | bytes 3145732
  0.0 6.3 %collective-permute-start.1 = (bf16[256,2048]{1,0:T(8,128)(2,1)}, bf16[256,2048]{1,0:T(8,128)(2,1)S(1)}, u32[]{:S(2)}, u32[]{:S(2)}) collective-permute-start(bf16[256,2048]{1,0:T(8,128)(2,1)} %own.1), channel_id=1, source_target_pairs={{0,1},{1,0},{2,3},{3,2},{4,5},{5,4},{6,7},{7,6},{8,9},{9,8},{10,11... | collective-permute-start | bytes 3145736 | tf_op jit(solution)/shard_map/ppermute | solution.py:378
  0.5 8.7 %collective-permute-start.3 = (bf16[4,16,2048]{2,1,0:T(8,128)(2,1)}, bf16[4,16,2048]{2,1,0:T(8,128)(2,1)S(1)}, u32[]{:S(2)}, u32[]{:S(2)}) collective-permute-start(bf16[4,16,2048]{2,1,0:T(8,128)(2,1)} %refs_0_.1), channel_id=1, source_target_pairs={{0,4},{1,3},{4,8},{5,1},{8,12},{9,5},{12,14},{13,9},{14,10},{15,13... | collective-permute-start | bytes 786440 | tf_op jit(solution)/shard_map/ppermute | solution.py:421
  3.1 9.0 %collective-permute-start = (bf16[4,16,2048]{2,1,0:T(8,128)(2,1)}, bf16[4,16,2048]{2,1,0:T(8,128)(2,1)S(1)}, u32[]{:S(2)}, u32[]{:S(2)}) collective-permute-start(bf16[4,16,2048]{2,1,0:T(8,128)(2,1)} %refs_0_.1), channel_id=1, source_target_pairs={{1,4},{0,3},{5,8},{4,1},{9,12},{8,5},{13,14},{12,9},{15,10},{14,13... | collective-permute-start | bytes 786440 | tf_op jit(solution)/shard_map/ppermute | solution.py:421
  5.1 1.2 %collective-permute-start.2 = (s32[4,128]{1,0:T(4,128)S(1)}, s32[4,128]{1,0:T(4,128)S(1)}, u32[]{:S(2)}, u32[]{:S(2)}) collective-permute-start(s32[4,128]{1,0:T(4,128)S(1)} %pad_add_fusion.notes), channel_id=1, source_target_pairs={{0,1},{1,0},{2,3},{3,2},{4,5},{5,4},{6,7},{7,6},{8,9},{9,8},{10,11... | collective-permute-start | bytes 6152 | tf_op jit(solution)/shard_map/ppermute | solution.py:378
  6.3 5.2 %copy-start.1 = (bf16[4,16,2048]{2,1,0:T(8,128)(2,1)S(1)}, bf16[4,16,2048]{2,1,0:T(8,128)(2,1)}, u32[]{:S(2)}) copy-start(bf16[4,16,2048]{2,1,0:T(8,128)(2,1)} %refs_0_.1) | copy-start | bytes 786436
  9.1 7.0 %collective-permute-start.5 = (bf16[4,16,2048]{2,1,0:T(8,128)(2,1)S(1)}, bf16[4,16,2048]{2,1,0:T(8,128)(2,1)S(1)}, u32[]{:S(2)}, u32[]{:S(2)}) collective-permute-start(bf16[4,16,2048]{2,1,0:T(8,128)(2,1)S(1)} %collective-permute-done.3.refs_0_), channel_id=1, source_target_pairs={{0,4},{1,3},{4,8},{5,1},{8,12},{9,5},{12,14},{13,9},{14,10},{15,13... | collective-permute-start | bytes 786440 | tf_op jit(solution)/shard_map/ppermute | solution.py:421
  12.1 5.8 %copy-start.2 = (f32[2,1024]{1,0:T(2,128)S(1)}, f32[2,1024]{1,0:T(2,128)}, u32[]{:S(2)}) copy-start(f32[2,1024]{1,0:T(2,128)} %filters.1) | copy-start | bytes 24580
  12.1 6.9 %collective-permute-start.4 = (bf16[4,16,2048]{2,1,0:T(8,128)(2,1)S(1)}, bf16[4,16,2048]{2,1,0:T(8,128)(2,1)S(1)}, u32[]{:S(2)}, u32[]{:S(2)}) collective-permute-start(bf16[4,16,2048]{2,1,0:T(8,128)(2,1)S(1)} %collective-permute-done.refs_1_), channel_id=1, source_target_pairs={{0,4},{1,3},{4,8},{5,1},{8,12},{9,5},{12,14},{13,9},{14,10},{15,13... | collective-permute-start | bytes 786440 | tf_op jit(solution)/shard_map/ppermute | solution.py:421
  16.1 6.4 %collective-permute-start.6 = (bf16[4,16,2048]{2,1,0:T(8,128)(2,1)S(1)}, bf16[4,16,2048]{2,1,0:T(8,128)(2,1)S(1)}, u32[]{:S(2)}, u32[]{:S(2)}) collective-permute-start(bf16[4,16,2048]{2,1,0:T(8,128)(2,1)S(1)} %collective-permute-done.5.refs_0_), channel_id=1, source_target_pairs={{0,4},{1,3},{4,8},{5,1},{8,12},{9,5},{12,14},{13,9},{14,10},{15,13... | collective-permute-start | bytes 786440 | tf_op jit(solution)/shard_map/ppermute | solution.py:421
  19.0 6.4 %collective-permute-start.8 = (bf16[4,16,2048]{2,1,0:T(8,128)(2,1)S(1)}, bf16[4,16,2048]{2,1,0:T(8,128)(2,1)S(1)}, u32[]{:S(2)}, u32[]{:S(2)}) collective-permute-start(bf16[4,16,2048]{2,1,0:T(8,128)(2,1)S(1)} %collective-permute-done.4.refs_1_), channel_id=1, source_target_pairs={{0,4},{1,3},{4,8},{5,1},{8,12},{9,5},{12,14},{13,9},{14,10},{15,13... | collective-permute-start | bytes 786440 | tf_op jit(solution)/shard_map/ppermute | solution.py:421
  22.5 6.4 %collective-permute-start.7 = (bf16[4,16,2048]{2,1,0:T(8,128)(2,1)S(1)}, bf16[4,16,2048]{2,1,0:T(8,128)(2,1)S(1)}, u32[]{:S(2)}, u32[]{:S(2)}) collective-permute-start(bf16[4,16,2048]{2,1,0:T(8,128)(2,1)S(1)} %collective-permute-done.6.refs_0_), channel_id=1, source_target_pairs={{0,4},{1,3},{4,8},{5,1},{8,12},{9,5},{12,14},{13,9},{14,10},{15,13... | collective-permute-start | bytes 786440 | tf_op jit(solution)/shard_map/ppermute | solution.py:421
  29.5 1.3 %collective-permute-start.9 = (f32[8,2048]{1,0:T(8,128)S(1)}, f32[8,2048]{1,0:T(8,128)S(1)}, u32[]{:S(2)}, u32[]{:S(2)}) collective-permute-start(f32[8,2048]{1,0:T(8,128)S(1)} %get-tuple-element.56), channel_id=1, source_target_pairs={{0,1},{1,0},{2,3},{3,2},{4,5},{5,4},{6,7},{7,6},{8,9},{9,8},{10,11... | collective-permute-start | bytes 196616 | tf_op jit(solution)/shard_map/ppermute | solution.py:378

commit v4 on v3

--- a/solution.py
+++ b/solution.py
@@ -257,11 +257,11 @@
     return values[0]
 
 
-def products_kernel(chunks, count, with_total, extra, *refs):
+def products_kernel(chunks, count, with_total, extra, shares, *refs):
     pieces = refs[:count]
     even, odd, spectra = refs[count : count + 3]
-    totals = refs[count + 3 : count + 3 + 2 * with_total]
-    outs = refs[count + 3 + 2 * with_total + extra : -1]
+    totals = refs[count + 3 : count + 3 + len(shares) * with_total]
+    outs = refs[count + 3 + len(shares) * with_total + extra : -1]
     work = refs[-1]
     samples = work.shape[1]
     number = spectra.shape[1]
@@ -272,15 +272,15 @@
     for block in transform(split(data), even, odd):
         work[:, first : first + block.shape[1]] = block
         first += block.shape[1]
-    if len(outs) > 2:
-        outs[2][...] = jnp.zeros(outs[2].shape, F32)
+    if len(outs) > len(shares):
+        outs[-1][...] = jnp.zeros(outs[-1].shape, F32)
     for start, distance, width in groups(samples):
         for block in range(width // 128):
             re = pl.ds(start + block * 128, 128)
             im = pl.ds(start + distance + block * 128, 128)
             sums = {}
             for c in range(len(chunks)):
-                for r in range(number):
+                for r in [i * (number // 2) + k for i in shares for k in range(number // 2)]:
                     right = [spectra[chunks[c], r, :, k].astype(F32) for k in (re, im)]
                     for h in range(ROWS // 8):
                         b_re, b_im = (b[8 * h : 8 * h + 8] for b in right)
@@ -293,13 +293,13 @@
                                 x, y = x + sums[s, r][0], y + sums[s, r][1]
                             sums[s, r] = (x, y)
             share = number // 2
-            for i in range(2):
+            for n, i in enumerate(shares):
                 keys = [(s, i * share + r) for r in range(share) for s in range(sources)]
                 for part, columns in enumerate((re, im)):
                     value = sum_rows([sums[key][part] for key in keys])
                     if with_total:
-                        value = value + totals[i][:, columns]
-                    outs[i][:, columns] = value
+                        value = value + totals[n][:, columns]
+                    outs[n][:, columns] = value
 
 
 def finish_kernel(scale, filters, mine, arrived, even, odd, out):
@@ -395,19 +395,19 @@
     def arrange(filters):
         return call(filters_kernel, [struct(filters.shape, F32)], "v")(filters)[0]
 
-    def add(pieces, numbers, totals, extra=(), mark=True):
+    def add(pieces, numbers, totals, extra=(), mark=True, shares=(0, 1)):
         kernel = functools.partial(
-            products_kernel, numbers, len(pieces), bool(totals), len(extra)
+            products_kernel, numbers, len(pieces), bool(totals), len(extra), shares
         )
         arguments = [*pieces, *tables, spectra, *totals, *extra]
         row_shape = struct((out_dev * sources, samples), F32)
         result = call(
             kernel,
-            [row_shape, row_shape, *[token] * mark],
+            [*[row_shape] * len(shares), *[token] * mark],
             "v" * len(arguments),
             [pltpu.VMEM((len(numbers) * sources * ROWS, samples), F32)],
         )(*arguments)
-        return result[:2], result[-1]
+        return result[: len(shares)], result[-1]
 
     if ringed:
         order = [0, 2, 4, 6, 7, 5, 3, 1]
@@ -435,7 +435,8 @@
         totals, _ = add([a2, b2], [3, 4], totals, [first, second], mark=False)
         a4 = send(a3)
         totals, _ = add([a3, b3], [5, 6], totals, mark=False)
-        (mine, theirs), _ = add([a4], [7], totals, mark=False)
+        (theirs,), _ = add([a4], [7], totals[1:], mark=False, shares=(1,))
+        (mine,), _ = add([a4], [7], totals[:1], mark=False, shares=(0,))
     else:
         spectra, _ = setup()
         gathered = lax.all_gather(source_traces, "rx", axis=1, tiled=True)

time: 31.9 us -> 31.7 us (level)
  waiting for transfers between devices: 6.87 us -> 6.43 us
    ppermute x7, waiting for transfers between devices: 5.78 us -> 5.44 us  [send(): return lax.ppermute(x, ('rx', 'xl'), pairs)]
    pallas_call x5 -> x6, Pallas kernels: 4.32 us -> 4.58 us  [add(): call(kernel, [*[row_shape] * len(shares), *[token] * mark], 'v' * len(arg...]
  transfers between devices with their start and end apart: 10 -> 10, of which waited for: 6 -> 5; matrix products, arithmetic and copies ran while one was open for 2% -> 2% of each run, Pallas kernels for 27% -> 29%
where the time goes in v4:
time: 31.7 us; the launch traced here: 31.6 us
  starting transfers between devices  13.9 us (44%)
  Pallas kernels  10.4 us (33%)
  waiting for transfers between devices  6.43 us (20%)
  other arithmetic  0.7 us (2%)
    ppermute x7, starting transfers between devices, send(): return lax.ppermute(x, ('rx', 'xl'), pairs)  12.9 us
    ppermute x7, waiting for transfers between devices, send(): return lax.ppermute(x, ('rx', 'xl'), pairs)  5.44 us
    pallas_call x6, Pallas kernels, add(): call(kernel, [*[row_shape] * len(shares), *[token] * mark], 'v' * len(arg...  4.58 us
    pallas_call x1, Pallas kernels, setup(): call(functools.partial(setup_kernel, own_traces, aper, ringed), [struct((...  2.82 us
    pallas_call x1, Pallas kernels, arrange(): return call(filters_kernel, [struct(filters.shape, F32)], 'v')(filters)[0]  1.12 us
    ppermute x3, waiting for transfers between devices, swap(): return lax.ppermute(x, 'xl', [(0, 1), (1, 0)])  0.99 us
    ppermute x3, starting transfers between devices, swap(): return lax.ppermute(x, 'xl', [(0, 1), (1, 0)])  0.94 us
    pallas_call x1, Pallas kernels, per_device(): call(functools.partial(finish_kernel, 1.0 / math.sqrt(aper)), [struct((so...  0.92 us
  transfers between devices with their start and end apart: 10, of which 5 were waited for; matrix products, arithmetic and copies ran while one was open for 2% of the time, Pallas kernels for 29%

profile of v4, /device:TPU:0, one launch (start us, length us, event | category | flops | bytes accessed | tf_op | source)
XLA Modules:
  0.0 31.6 jit_solution(12620788314817057834)
XLA Ops:
  0.0 0.0 copy-start
  0.0 0.5 %collective-permute-start.1 = (bf16[256,2048]{1,0:T(8,128)(2,1)}, bf16[256,2048]{1,0:T(8,128)(2,1)S(1)}, u32[]{:S(2)}, u32[]{:S(2)}) collective-permute-start(bf16[256,2048]{1,0:T(8,128)(2,1)} %own.1), channel_id=1, source_target_pairs={{0,1},{1,0},{2,3},{3,2},{4,5},{5,4},{6,7},{7,6},{8,9},{9,8},{10,11... | collective-permute-start | bytes 3145736 | tf_op jit(solution)/shard_map/ppermute | solution.py:378
  0.5 2.6 %collective-permute-start.3 = (bf16[4,16,2048]{2,1,0:T(8,128)(2,1)}, bf16[4,16,2048]{2,1,0:T(8,128)(2,1)S(1)}, u32[]{:S(2)}, u32[]{:S(2)}) collective-permute-start(bf16[4,16,2048]{2,1,0:T(8,128)(2,1)} %refs_0_.1), channel_id=1, source_target_pairs={{0,4},{1,3},{4,8},{5,1},{8,12},{9,5},{12,14},{13,9},{14,10},{15,13... | collective-permute-start | bytes 786440 | tf_op jit(solution)/shard_map/ppermute | solution.py:421
  3.1 1.3 %collective-permute-start = (bf16[4,16,2048]{2,1,0:T(8,128)(2,1)}, bf16[4,16,2048]{2,1,0:T(8,128)(2,1)S(1)}, u32[]{:S(2)}, u32[]{:S(2)}) collective-permute-start(bf16[4,16,2048]{2,1,0:T(8,128)(2,1)} %refs_0_.1), channel_id=1, source_target_pairs={{1,4},{0,3},{5,8},{4,1},{9,12},{8,5},{13,14},{12,9},{15,10},{14,13... | collective-permute-start | bytes 786440 | tf_op jit(solution)/shard_map/ppermute | solution.py:421
  4.4 0.7 %pad_add_fusion.notes = s32[4,128]{1,0:T(4,128)S(1)} fusion(s32[2,128]{1,0:T(2,128)} %param.9, s32[2,128]{1,0:T(2,128)} %bitcast.3), kind=kLoop, calls=%fused_computation | loop fusion | flops 512 | bytes 4096 | tf_op jit(solution)/shard_map/concatenate | solution.py:380
  5.1 0.4 %collective-permute-start.2 = (s32[4,128]{1,0:T(4,128)S(1)}, s32[4,128]{1,0:T(4,128)S(1)}, u32[]{:S(2)}, u32[]{:S(2)}) collective-permute-start(s32[4,128]{1,0:T(4,128)S(1)} %pad_add_fusion.notes), channel_id=1, source_target_pairs={{0,1},{1,0},{2,3},{3,2},{4,5},{5,4},{6,7},{7,6},{8,9},{9,8},{10,11... | collective-permute-start | bytes 6152 | tf_op jit(solution)/shard_map/ppermute | solution.py:378
  5.5 0.6 %shard_map.55 = (bf16[2,256,256]{2,1,0:T(8,128)(2,1)S(1)}, bf16[3,256,512]{2,1,0:T(8,128)(2,1)S(1)}) custom-call(s32[1]{0:T(128)} %bitcast.rx, s32[1]{0:T(128)} %bitcast.1.xl.place), custom_call_target="tpu_custom_call" | custom-call | flops 1000000000 | bytes 3000000 | tf_op jit(solution)/shard_map/pallas_call | solution.py:383
  6.1 0.2 collective-permute-done.2.notes_other
  6.3 0.0 collective-permute-done.1.other
  6.3 0.0 copy-done
  6.3 0.0 copy-start.1
  6.3 2.8 %shard_map.56 = (bf16[8,4,16,2048]{3,2,1,0:T(8,128)(2,1)S(1)}, f32[8,128]{1,0:T(8,128)S(1)}) custom-call(s32[1]{0:T(128)} %bitcast.rx, s32[1]{0:T(128)} %bitcast.1.xl.place, bf16[256,2048]{1,0:T(8,128)(2,1)S(1)} %copy-done, bf16[256,2048]{1,0:T(8,128)(2,1)S(1)} %collective-permute-done.1.other, s32[4,128]{1,0:T(4,128)S(1)} %pad_add_fusion.notes, ...), custom_call_target="tpu_custom_call" | custom-call | flops 4000000000 | bytes 12000000 | tf_op jit(solution)/shard_map/pallas_call | solution.py:388
  9.1 0.0 collective-permute-done.3.refs_0_
  9.1 2.3 %collective-permute-start.5 = (bf16[4,16,2048]{2,1,0:T(8,128)(2,1)S(1)}, bf16[4,16,2048]{2,1,0:T(8,128)(2,1)S(1)}, u32[]{:S(2)}, u32[]{:S(2)}) collective-permute-start(bf16[4,16,2048]{2,1,0:T(8,128)(2,1)S(1)} %collective-permute-done.3.refs_0_), channel_id=1, source_target_pairs={{0,4},{1,3},{4,8},{5,1},{8,12},{9,5},{12,14},{13,9},{14,10},{15,13... | collective-permute-start | bytes 786440 | tf_op jit(solution)/shard_map/ppermute | solution.py:421
  11.5 0.0 copy-done.1
  11.5 0.6 %shard_map.57 = (f32[8,2048]{1,0:T(8,128)S(1)}, f32[8,2048]{1,0:T(8,128)S(1)}, f32[8,128]{1,0:T(8,128)S(1)}) custom-call(bf16[4,16,2048]{2,1,0:T(8,128)(2,1)S(1)} %copy-done.1, bf16[2,256,256]{2,1,0:T(8,128)(2,1)S(1)} %get-tuple-element.30.even.refs_1_.refs_2_, bf16[3,256,512]{2,1,0:T(8,128)(2,1)S(1)} %get-tuple-element.31.odd.refs_2_.refs_3_, ...), custom_call_target="tpu_custom_call" | custom-call | flops 1000000000 | bytes 3000000 | tf_op jit(solution)/shard_map/pallas_call | solution.py:404
  12.1 0.0 copy-start.2
  12.1 0.0 collective-permute-done.refs_1_
  12.1 1.6 %collective-permute-start.4 = (bf16[4,16,2048]{2,1,0:T(8,128)(2,1)S(1)}, bf16[4,16,2048]{2,1,0:T(8,128)(2,1)S(1)}, u32[]{:S(2)}, u32[]{:S(2)}) collective-permute-start(bf16[4,16,2048]{2,1,0:T(8,128)(2,1)S(1)} %collective-permute-done.refs_1_), channel_id=1, source_target_pairs={{0,4},{1,3},{4,8},{5,1},{8,12},{9,5},{12,14},{13,9},{14,10},{15,13... | collective-permute-start | bytes 786440 | tf_op jit(solution)/shard_map/ppermute | solution.py:421
  13.7 1.0 %shard_map.59 = (f32[8,2048]{1,0:T(8,128)S(1)}, f32[8,2048]{1,0:T(8,128)S(1)}, f32[8,128]{1,0:T(8,128)S(1)}) custom-call(bf16[4,16,2048]{2,1,0:T(8,128)(2,1)S(1)} %collective-permute-done.3.refs_0_, bf16[4,16,2048]{2,1,0:T(8,128)(2,1)S(1)} %collective-permute-done.refs_1_, bf16[2,256,256]{2,1,0:T(8,128)(2,1)S(1)} %get-tuple-element.30.even.refs_1_.refs_2_, ...), custom_call_target="tpu_custom_call" | custom-call | flops 1000000000 | bytes 3000000 | tf_op jit(solution)/shard_map/pallas_call | solution.py:404
  14.8 1.4 %collective-permute-done.5.refs_0_ = bf16[4,16,2048]{2,1,0:T(8,128)(2,1)S(1)} collective-permute-done((bf16[4,16,2048]{2,1,0:T(8,128)(2,1)S(1)}, bf16[4,16,2048]{2,1,0:T(8,128)(2,1)S(1)}, u32[]{:S(2)}, u32[]{:S(2)}) %collective-permute-start.5) | collective-permute-done | bytes 262176 | tf_op jit(solution)/shard_map/ppermute | solution.py:421
  16.1 1.7 %collective-permute-start.6 = (bf16[4,16,2048]{2,1,0:T(8,128)(2,1)S(1)}, bf16[4,16,2048]{2,1,0:T(8,128)(2,1)S(1)}, u32[]{:S(2)}, u32[]{:S(2)}) collective-permute-start(bf16[4,16,2048]{2,1,0:T(8,128)(2,1)S(1)} %collective-permute-done.5.refs_0_), channel_id=1, source_target_pairs={{0,4},{1,3},{4,8},{5,1},{8,12},{9,5},{12,14},{13,9},{14,10},{15,13... | collective-permute-start | bytes 786440 | tf_op jit(solution)/shard_map/ppermute | solution.py:421
  17.8 0.0 copy-done.2
  17.8 1.1 %shard_map.58.filters = f32[2,1024]{1,0:T(2,128)S(1)} custom-call(f32[2,1024]{1,0:T(2,128)S(1)} %copy-done.2), custom_call_target="tpu_custom_call" | custom-call | flops 1000000000 | bytes 3000000 | tf_op jit(solution)/shard_map/pallas_call | solution.py:396
  19.0 0.0 collective-permute-done.4.refs_1_
  19.0 1.7 %collective-permute-start.8 = (bf16[4,16,2048]{2,1,0:T(8,128)(2,1)S(1)}, bf16[4,16,2048]{2,1,0:T(8,128)(2,1)S(1)}, u32[]{:S(2)}, u32[]{:S(2)}) collective-permute-start(bf16[4,16,2048]{2,1,0:T(8,128)(2,1)S(1)} %collective-permute-done.4.refs_1_), channel_id=1, source_target_pairs={{0,4},{1,3},{4,8},{5,1},{8,12},{9,5},{12,14},{13,9},{14,10},{15,13... | collective-permute-start | bytes 786440 | tf_op jit(solution)/shard_map/ppermute | solution.py:421
  20.6 1.9 %collective-permute-done.6.refs_0_ = bf16[4,16,2048]{2,1,0:T(8,128)(2,1)S(1)} collective-permute-done((bf16[4,16,2048]{2,1,0:T(8,128)(2,1)S(1)}, bf16[4,16,2048]{2,1,0:T(8,128)(2,1)S(1)}, u32[]{:S(2)}, u32[]{:S(2)}) %collective-permute-start.6) | collective-permute-done | bytes 262176 | tf_op jit(solution)/shard_map/ppermute | solution.py:421
  22.5 1.7 %collective-permute-start.7 = (bf16[4,16,2048]{2,1,0:T(8,128)(2,1)S(1)}, bf16[4,16,2048]{2,1,0:T(8,128)(2,1)S(1)}, u32[]{:S(2)}, u32[]{:S(2)}) collective-permute-start(bf16[4,16,2048]{2,1,0:T(8,128)(2,1)S(1)} %collective-permute-done.6.refs_0_), channel_id=1, source_target_pairs={{0,4},{1,3},{4,8},{5,1},{8,12},{9,5},{12,14},{13,9},{14,10},{15,13... | collective-permute-start | bytes 786440 | tf_op jit(solution)/shard_map/ppermute | solution.py:421
  24.2 0.3 %shard_map.64 = (bf16[2,256,256]{2,1,0:T(8,128)(2,1)S(1)}, bf16[3,256,512]{2,1,0:T(8,128)(2,1)S(1)}) custom-call(), custom_call_target="tpu_custom_call" | custom-call | flops 1000000000 | bytes 3000000 | tf_op jit(solution)/shard_map/pallas_call | solution.py:451
  24.5 1.0 %shard_map.60 = (f32[8,2048]{1,0:T(8,128)S(1)}, f32[8,2048]{1,0:T(8,128)S(1)}) custom-call(bf16[4,16,2048]{2,1,0:T(8,128)(2,1)S(1)} %collective-permute-done.5.refs_0_, bf16[4,16,2048]{2,1,0:T(8,128)(2,1)S(1)} %collective-permute-done.4.refs_1_, bf16[2,256,256]{2,1,0:T(8,128)(2,1)S(1)} %get-tuple-element.30.even.refs_1_.refs_2_, ...), custom_call_target="tpu_custom_call" | custom-call | flops 1000000000 | bytes 3000000 | tf_op jit(solution)/shard_map/pallas_call | solution.py:404
  25.6 0.0 collective-permute-done.8.refs_1_
  25.6 1.0 %shard_map.61 = (f32[8,2048]{1,0:T(8,128)S(1)}, f32[8,2048]{1,0:T(8,128)S(1)}) custom-call(bf16[4,16,2048]{2,1,0:T(8,128)(2,1)S(1)} %collective-permute-done.6.refs_0_, bf16[4,16,2048]{2,1,0:T(8,128)(2,1)S(1)} %collective-permute-done.8.refs_1_, bf16[2,256,256]{2,1,0:T(8,128)(2,1)S(1)} %get-tuple-element.30.even.refs_1_.refs_2_, ...), custom_call_target="tpu_custom_call" | custom-call | flops 1000000000 | bytes 3000000 | tf_op jit(solution)/shard_map/pallas_call | solution.py:404
  26.7 2.2 %collective-permute-done.7.refs_0_ = bf16[4,16,2048]{2,1,0:T(8,128)(2,1)S(1)} collective-permute-done((bf16[4,16,2048]{2,1,0:T(8,128)(2,1)S(1)}, bf16[4,16,2048]{2,1,0:T(8,128)(2,1)S(1)}, u32[]{:S(2)}, u32[]{:S(2)}) %collective-permute-start.7) | collective-permute-done | bytes 262176 | tf_op jit(solution)/shard_map/ppermute | solution.py:421
  28.9 0.4 %shard_map.63 = f32[8,2048]{1,0:T(8,128)S(1)} custom-call(bf16[4,16,2048]{2,1,0:T(8,128)(2,1)S(1)} %collective-permute-done.7.refs_0_, bf16[2,256,256]{2,1,0:T(8,128)(2,1)S(1)} %get-tuple-element.30.even.refs_1_.refs_2_, bf16[3,256,512]{2,1,0:T(8,128)(2,1)S(1)} %get-tuple-element.31.odd.refs_2_.refs_3_, ...), custom_call_target="tpu_custom_call" | custom-call | flops 1000000000 | bytes 3000000 | tf_op jit(solution)/shard_map/pallas_call | solution.py:404
  29.3 0.1 collective-permute-start.9
  29.4 0.4 %shard_map.62.mine = f32[8,2048]{1,0:T(8,128)S(1)} custom-call(bf16[4,16,2048]{2,1,0:T(8,128)(2,1)S(1)} %collective-permute-done.7.refs_0_, bf16[2,256,256]{2,1,0:T(8,128)(2,1)S(1)} %get-tuple-element.30.even.refs_1_.refs_2_, bf16[3,256,512]{2,1,0:T(8,128)(2,1)S(1)} %get-tuple-element.31.odd.refs_2_.refs_3_, ...), custom_call_target="tpu_custom_call" | custom-call | flops 1000000000 | bytes 3000000 | tf_op jit(solution)/shard_map/pallas_call | solution.py:404
  29.8 0.8 %collective-permute-done.9.arrived = f32[8,2048]{1,0:T(8,128)S(1)} collective-permute-done((f32[8,2048]{1,0:T(8,128)S(1)}, f32[8,2048]{1,0:T(8,128)S(1)}, u32[]{:S(2)}, u32[]{:S(2)}) %collective-permute-start.9) | collective-permute-done | bytes 65568 | tf_op jit(solution)/shard_map/ppermute | solution.py:378
  30.6 0.9 %shard_map.65 = bf16[4,2,2048]{2,1,0:T(2,128)(2,1)} custom-call(f32[2,1024]{1,0:T(2,128)S(1)} %shard_map.58.filters, f32[8,2048]{1,0:T(8,128)S(1)} %shard_map.62.mine, f32[8,2048]{1,0:T(8,128)S(1)} %collective-permute-done.9.arrived, bf16[2,256,256]{2,1,0:T(8,128)(2,1)S(1)} %get-tuple-element.53.even, bf16[3,256,512]{2,1,0:T(8,128)(2,1)S(1)} %get-tuple-element.54.odd), custom_call_target="tpu_custom_call" | custom-call | flops 1000000000 | bytes 3000000 | tf_op jit(solution)/shard_map/pallas_call | solution.py:452
Async XLA Ops:
  0.0 6.3 %copy-start = (bf16[256,2048]{1,0:T(8,128)(2,1)S(1)}, bf16[256,2048]{1,0:T(8,128)(2,1)}, u32[]{:S(2)}) copy-start(bf16[256,2048]{1,0:T(8,128)(2,1)} %own.1) | copy-start | bytes 3145732
  0.0 6.3 %collective-permute-start.1 = (bf16[256,2048]{1,0:T(8,128)(2,1)}, bf16[256,2048]{1,0:T(8,128)(2,1)S(1)}, u32[]{:S(2)}, u32[]{:S(2)}) collective-permute-start(bf16[256,2048]{1,0:T(8,128)(2,1)} %own.1), channel_id=1, source_target_pairs={{0,1},{1,0},{2,3},{3,2},{4,5},{5,4},{6,7},{7,6},{8,9},{9,8},{10,11... | collective-permute-start | bytes 3145736 | tf_op jit(solution)/shard_map/ppermute | solution.py:378
  0.5 8.7 %collective-permute-start.3 = (bf16[4,16,2048]{2,1,0:T(8,128)(2,1)}, bf16[4,16,2048]{2,1,0:T(8,128)(2,1)S(1)}, u32[]{:S(2)}, u32[]{:S(2)}) collective-permute-start(bf16[4,16,2048]{2,1,0:T(8,128)(2,1)} %refs_0_.1), channel_id=1, source_target_pairs={{0,4},{1,3},{4,8},{5,1},{8,12},{9,5},{12,14},{13,9},{14,10},{15,13... | collective-permute-start | bytes 786440 | tf_op jit(solution)/shard_map/ppermute | solution.py:421
  3.1 9.0 %collective-permute-start = (bf16[4,16,2048]{2,1,0:T(8,128)(2,1)}, bf16[4,16,2048]{2,1,0:T(8,128)(2,1)S(1)}, u32[]{:S(2)}, u32[]{:S(2)}) collective-permute-start(bf16[4,16,2048]{2,1,0:T(8,128)(2,1)} %refs_0_.1), channel_id=1, source_target_pairs={{1,4},{0,3},{5,8},{4,1},{9,12},{8,5},{13,14},{12,9},{15,10},{14,13... | collective-permute-start | bytes 786440 | tf_op jit(solution)/shard_map/ppermute | solution.py:421
  5.1 1.2 %collective-permute-start.2 = (s32[4,128]{1,0:T(4,128)S(1)}, s32[4,128]{1,0:T(4,128)S(1)}, u32[]{:S(2)}, u32[]{:S(2)}) collective-permute-start(s32[4,128]{1,0:T(4,128)S(1)} %pad_add_fusion.notes), channel_id=1, source_target_pairs={{0,1},{1,0},{2,3},{3,2},{4,5},{5,4},{6,7},{7,6},{8,9},{9,8},{10,11... | collective-permute-start | bytes 6152 | tf_op jit(solution)/shard_map/ppermute | solution.py:378
  6.3 5.2 %copy-start.1 = (bf16[4,16,2048]{2,1,0:T(8,128)(2,1)S(1)}, bf16[4,16,2048]{2,1,0:T(8,128)(2,1)}, u32[]{:S(2)}) copy-start(bf16[4,16,2048]{2,1,0:T(8,128)(2,1)} %refs_0_.1) | copy-start | bytes 786436
  9.1 7.0 %collective-permute-start.5 = (bf16[4,16,2048]{2,1,0:T(8,128)(2,1)S(1)}, bf16[4,16,2048]{2,1,0:T(8,128)(2,1)S(1)}, u32[]{:S(2)}, u32[]{:S(2)}) collective-permute-start(bf16[4,16,2048]{2,1,0:T(8,128)(2,1)S(1)} %collective-permute-done.3.refs_0_), channel_id=1, source_target_pairs={{0,4},{1,3},{4,8},{5,1},{8,12},{9,5},{12,14},{13,9},{14,10},{15,13... | collective-permute-start | bytes 786440 | tf_op jit(solution)/shard_map/ppermute | solution.py:421
  12.1 5.8 %copy-start.2 = (f32[2,1024]{1,0:T(2,128)S(1)}, f32[2,1024]{1,0:T(2,128)}, u32[]{:S(2)}) copy-start(f32[2,1024]{1,0:T(2,128)} %filters.1) | copy-start | bytes 24580
  12.1 6.9 %collective-permute-start.4 = (bf16[4,16,2048]{2,1,0:T(8,128)(2,1)S(1)}, bf16[4,16,2048]{2,1,0:T(8,128)(2,1)S(1)}, u32[]{:S(2)}, u32[]{:S(2)}) collective-permute-start(bf16[4,16,2048]{2,1,0:T(8,128)(2,1)S(1)} %collective-permute-done.refs_1_), channel_id=1, source_target_pairs={{0,4},{1,3},{4,8},{5,1},{8,12},{9,5},{12,14},{13,9},{14,10},{15,13... | collective-permute-start | bytes 786440 | tf_op jit(solution)/shard_map/ppermute | solution.py:421
  16.1 6.4 %collective-permute-start.6 = (bf16[4,16,2048]{2,1,0:T(8,128)(2,1)S(1)}, bf16[4,16,2048]{2,1,0:T(8,128)(2,1)S(1)}, u32[]{:S(2)}, u32[]{:S(2)}) collective-permute-start(bf16[4,16,2048]{2,1,0:T(8,128)(2,1)S(1)} %collective-permute-done.5.refs_0_), channel_id=1, source_target_pairs={{0,4},{1,3},{4,8},{5,1},{8,12},{9,5},{12,14},{13,9},{14,10},{15,13... | collective-permute-start | bytes 786440 | tf_op jit(solution)/shard_map/ppermute | solution.py:421
  19.0 6.6 %collective-permute-start.8 = (bf16[4,16,2048]{2,1,0:T(8,128)(2,1)S(1)}, bf16[4,16,2048]{2,1,0:T(8,128)(2,1)S(1)}, u32[]{:S(2)}, u32[]{:S(2)}) collective-permute-start(bf16[4,16,2048]{2,1,0:T(8,128)(2,1)S(1)} %collective-permute-done.4.refs_1_), channel_id=1, source_target_pairs={{0,4},{1,3},{4,8},{5,1},{8,12},{9,5},{12,14},{13,9},{14,10},{15,13... | collective-permute-start | bytes 786440 | tf_op jit(solution)/shard_map/ppermute | solution.py:421
  22.5 6.4 %collective-permute-start.7 = (bf16[4,16,2048]{2,1,0:T(8,128)(2,1)S(1)}, bf16[4,16,2048]{2,1,0:T(8,128)(2,1)S(1)}, u32[]{:S(2)}, u32[]{:S(2)}) collective-permute-start(bf16[4,16,2048]{2,1,0:T(8,128)(2,1)S(1)} %collective-permute-done.6.refs_0_), channel_id=1, source_target_pairs={{0,4},{1,3},{4,8},{5,1},{8,12},{9,5},{12,14},{13,9},{14,10},{15,13... | collective-permute-start | bytes 786440 | tf_op jit(solution)/shard_map/ppermute | solution.py:421
  29.3 1.3 %collective-permute-start.9 = (f32[8,2048]{1,0:T(8,128)S(1)}, f32[8,2048]{1,0:T(8,128)S(1)}, u32[]{:S(2)}, u32[]{:S(2)}) collective-permute-start(f32[8,2048]{1,0:T(8,128)S(1)} %shard_map.63), channel_id=1, source_target_pairs={{0,1},{1,0},{2,3},{3,2},{4,5},{5,4},{6,7},{7,6},{8,9},{9,8},{10,11... | collective-permute-start | bytes 196616 | tf_op jit(solution)/shard_map/ppermute | solution.py:378
